TPU v7x, 32 devices: a whole 2x2x4 slice. The times are simulated.
32 devices in a mesh: dp: 16 (over z, y, x), mp: 2 (over core).
Axes of the slice: x: 2, y: 2, z: 4, core: 2. Of those that a mesh axis runs over, the one named last changes fastest.
Arguments:
- tokens: bfloat16 [32768, 768], P('dp'), may hold values from -6 to 6
- cond: bfloat16 [32768, 128], P('dp'), may hold values from -6 to 6
- segments: int32 [32, 1024], P('dp'), may hold values from 0 to 3, never falling along the last dimension, each value on 1 to 512 neighbouring positions
- out_grad: bfloat16 [32768, 768], P('dp'), may hold values from -6 to 6
- step: int32 [1], replicated, may hold values from 2 to 20
- ada_weight: float32 [128, 4608], P(None, 'dp'), may hold values from -0.5 to 0.5
- ada_first: float32 [128, 4608], P(None, 'dp'), may hold values from -0.00061035156 to 0.00061035156
- ada_second: float32 [128, 4608], P(None, 'dp'), may hold values from 1.3031258e-10 to 5.212503e-10
- norm_params: float32 [8, 768], P(None, 'dp'), may hold values from 0.5 to 1.5
- norm_first: float32 [8, 768], P(None, 'dp'), may hold values from -0.0024414062 to 0.0024414062
- norm_second: float32 [8, 768], P(None, 'dp'), may hold values from 2.6062516e-10 to 1.0425006e-09
- qkv_weight: float32 [3, 768, 768], P(None, 'dp', 'mp'), may hold values from -0.109375 to 0.109375
- qkv_first: float32 [3, 768, 768], P(None, 'dp', 'mp'), may hold values from -0.00061035156 to 0.00061035156
- qkv_second: float32 [3, 768, 768], P(None, 'dp', 'mp'), may hold values from 1.3031258e-10 to 5.212503e-10
- out_weight: float32 [768, 768], P('mp', 'dp'), may hold values from -1.75 to 1.75
- out_first: float32 [768, 768], P('mp', 'dp'), may hold values from -0.00061035156 to 0.00061035156
- out_second: float32 [768, 768], P('mp', 'dp'), may hold values from 1.6289073e-11 to 6.515629e-11
- up_weight: float32 [768, 3072], P('dp', 'mp'), may hold values from -0.21875 to 0.21875
- up_first: float32 [768, 3072], P('dp', 'mp'), may hold values from -0.00061035156 to 0.00061035156
- up_second: float32 [768, 3072], P('dp', 'mp'), may hold values from 1.3031258e-10 to 5.212503e-10
- down_weight: float32 [3072, 768], P('mp', 'dp'), may hold values from -0.109375 to 0.109375
- down_first: float32 [3072, 768], P('mp', 'dp'), may hold values from -0.00061035156 to 0.00061035156
- down_second: float32 [3072, 768], P('mp', 'dp'), may hold values from 1.3031258e-10 to 5.212503e-10
Outputs:
- result: bfloat16 [32768, 768], P('dp')
- input_grad: float32 [32768, 768], P('dp')
- grad_norm: float32 [1], replicated
- ada_weight_next: float32 [128, 4608], P(None, 'dp')
- ada_first_next: float32 [128, 4608], P(None, 'dp')
- ada_second_next: float32 [128, 4608], P(None, 'dp')
- norm_params_next: float32 [8, 768], P(None, 'dp')
- norm_first_next: float32 [8, 768], P(None, 'dp')
- norm_second_next: float32 [8, 768], P(None, 'dp')
- qkv_weight_next: float32 [3, 768, 768], P(None, 'dp', 'mp')
- qkv_first_next: float32 [3, 768, 768], P(None, 'dp', 'mp')
- qkv_second_next: float32 [3, 768, 768], P(None, 'dp', 'mp')
- out_weight_next: float32 [768, 768], P('mp', 'dp')
- out_first_next: float32 [768, 768], P('mp', 'dp')
- out_second_next: float32 [768, 768], P('mp', 'dp')
- up_weight_next: float32 [768, 3072], P('dp', 'mp')
- up_first_next: float32 [768, 3072], P('dp', 'mp')
- up_second_next: float32 [768, 3072], P('dp', 'mp')
- down_weight_next: float32 [3072, 768], P('mp', 'dp')
- down_first_next: float32 [3072, 768], P('mp', 'dp')
- down_second_next: float32 [3072, 768], P('mp', 'dp')
Inputs may be any that keep to these rules, and one draw needn't show every extreme that they name: `segments`: along each sequence document ids never fall; each document holds 1 to 512 positions, and one document of a sequence holds exactly 512.
All inputs are finite; a program needn't handle non-finite values.
Results may differ from a plain program's by a relative error of at most 0.012.
The roundings to bfloat16 on the way count: a program that leaves them out, or rounds other values in their place, can miss the bound.
Values may be sent and summed in bfloat16 or wider, within the bound.
A program may use at most 320 MiB of HBM per device.

v0:
```python
import functools
import math

import jax
import jax.numpy as jnp
import numpy as np
from jax import lax
from jax.experimental import pallas as pl
from jax.experimental.pallas import tpu as pltpu
from jax.sharding import PartitionSpec as P

HEAD_DIM = 64
LANES = 128
MASKED = -1e30
ROW_BLOCK = 256
VMEM_LIMIT = 64_000_000
clip_limit = 1.0
step_rates = (0.075, 0.75, 0.075, 0.25, 0.075, 0.075)
decay_rates = (0.01, 0.0, 0.01, 0.01, 0.01, 0.01)

F32 = jnp.float32
BF = jnp.bfloat16
NN = (((1,), (0,)), ((), ()))
NT = (((1,), (1,)), ((), ()))


def dot(left, right, dims=NN):
    return lax.dot_general(left, right, dims, preferred_element_type=F32)


def shape_of(shape, dtype):
    return jax.ShapeDtypeStruct(shape, dtype)


def resident(shape, index):
    return pl.BlockSpec(shape, lambda *_: index, pipeline_mode=pl.Buffered(1))


def params():
    return pltpu.CompilerParams(vmem_limit_bytes=VMEM_LIMIT)


def adam_update(weight, first, second, grad, clip_factor, fix_one, fix_two, rate, decay):
    clipped = grad * clip_factor
    first_new = 0.9 * first + 0.1 * clipped
    second_new = 0.999 * second + 0.001 * clipped * clipped
    update = first_new / fix_one / (jnp.sqrt(second_new / fix_two) + 1e-08) + decay * weight
    return (weight - rate * update, first_new, second_new)


def rope_tables(length):
    half = HEAD_DIM // 2
    inverse = jnp.exp(jnp.arange(half, dtype=F32) * (-2.0 * math.log(10000.0) / HEAD_DIM))
    angles = jnp.arange(length, dtype=F32)[:, None] * inverse[None, :]
    cosines, sines = jnp.cos(angles), jnp.sin(angles)
    return (
        jnp.concatenate([cosines] * 4, axis=1),
        jnp.concatenate([-sines, sines, -sines, sines], axis=1),
    )


def rope_constants(length, fine=32):
    half = HEAD_DIM // 2
    inverse = np.exp(np.arange(half) * (-2.0 * math.log(10000.0) / HEAD_DIM))
    sign = np.repeat([-1.0, 1.0, -1.0, 1.0], half)
    tables = []
    for positions in (np.arange(0, length, fine), np.arange(fine)):
        angles = np.tile(positions[:, None] * inverse[None, :], (1, 4))
        tables += [np.cos(angles), np.sin(angles) * sign]
    return [jnp.asarray(table, F32) for table in tables]


def swap_halves(values):
    width = values.shape[1]
    lane = lax.broadcasted_iota(jnp.int32, values.shape, 1)
    ahead = pltpu.roll(values, width - HEAD_DIM // 2, 1)
    behind = pltpu.roll(values, HEAD_DIM // 2, 1)
    return jnp.where(lane % HEAD_DIM < HEAD_DIM // 2, ahead, behind)


def silu_low(cond):
    value = cond.astype(F32)
    return (value / (1.0 + jnp.exp(-value))).astype(BF)


def normalize(rows):
    centre = rows - jnp.mean(rows, axis=-1, keepdims=True)
    scale = lax.rsqrt(jnp.mean(centre * centre, axis=-1, keepdims=True) + 1e-05)
    return centre * scale, scale


def norm_backward(grad, normal, scale):
    return scale * (
        grad
        - jnp.mean(grad, axis=-1, keepdims=True)
        - normal * jnp.mean(grad * normal, axis=-1, keepdims=True)
    )


def cond_rows(cond):
    return jnp.concatenate([cond.T, jnp.ones((16, cond.shape[0]), BF)], axis=0)


def first_kernel(half, x_ref, c_ref, wa_ref, p_ref, wqa_ref, wqb_ref, cos_ref, sin_ref,
                 h_ref, q_ref, k_ref, v_ref):
    width = x_ref.shape[1]
    own = width // 2
    cond = silu_low(c_ref[...])
    mod = dot(cond, wa_ref[0 : 2 * width, :], NT)
    shift = mod[:, :width] + p_ref[2:3, :]
    scale = mod[:, width:] + p_ref[3:4, :]
    normal, _ = normalize(x_ref[...].astype(F32))
    h = (normal * p_ref[0:1, :] * (1.0 + scale) + shift).astype(BF)
    h_ref[...] = h
    cos = jnp.concatenate([cos_ref[...]] * (own // LANES), axis=1)
    sin = jnp.concatenate([sin_ref[...]] * (own // LANES), axis=1)
    for start, w_ref in ((0, wqa_ref), (own, wqb_ref)):
        cols = slice(start, start + own)
        query = dot(h, w_ref[:, 0:own])
        query = query * cos + swap_halves(query) * sin
        q_ref[:, cols] = (query * HEAD_DIM**-0.5).astype(BF)
        key = dot(h, w_ref[:, own : 2 * own])
        k_ref[:, cols] = (key * cos + swap_halves(key) * sin).astype(BF)
        v_ref[:, cols] = dot(h, w_ref[:, 2 * own :]).astype(BF)


def first_stage(half, tokens, cond, wa, norms, near, far, tables):
    width = tokens.shape[1]
    rows = tables[0].shape[0]
    blocks = rows // ROW_BLOCK
    mine = lambda i, half: (half[0] * blocks + i, 0)
    plain = lambda i, half: (i, 0)
    row = pl.BlockSpec((ROW_BLOCK, width), plain)
    return pl.pallas_call(
        first_kernel,
        grid_spec=pltpu.PrefetchScalarGridSpec(
            num_scalar_prefetch=1,
            grid=(blocks,),
            in_specs=[
                pl.BlockSpec((ROW_BLOCK, width), mine),
                pl.BlockSpec((ROW_BLOCK, cond.shape[1]), mine),
                resident(wa.shape, (0, 0)),
                resident(norms.shape, (0, 0)),
                resident((width, 3 * width // 2), (0, 0)),
                resident((width, 3 * width // 2), (0, 0)),
                pl.BlockSpec((ROW_BLOCK, LANES), plain),
                pl.BlockSpec((ROW_BLOCK, LANES), plain),
            ],
            out_specs=[row] * 4,
        ),
        out_shape=[shape_of((rows, width), BF)] * 4,
        compiler_params=params(),
        name="first_stage",
    )(half, tokens, cond, wa, norms, near, far, *tables)


def split_heads(pair, other):
    low = lax.broadcasted_iota(jnp.int32, pair.shape, 1) < HEAD_DIM
    return jnp.where(low, pair, other), jnp.where(low, other, pair)


def attend_kernel(lo_ref, hi_ref, q_ref, k_ref, v_ref, fq_ref, fk_ref, o_ref, lse_ref,
                  qz, kz, vt, *, bq, bk):
    length = q_ref.shape[0]
    qz[0], qz[1] = split_heads(q_ref[...], fq_ref[...])
    kz[0], kz[1] = split_heads(k_ref[...], fk_ref[...])
    vt[...] = v_ref[...].T

    def query_block(i, _):
        off = pl.multiple_of(i * bq, bq)
        queries = [qz[h, pl.ds(off, bq), :] for h in range(2)]

        def key_block(j, carry):
            koff = pl.multiple_of(j * bk, bk)
            scores = [dot(kz[h, pl.ds(koff, bk), :], queries[h], NT) for h in range(2)]
            out = []
            for h in range(2):
                top, total, mixed = carry[3 * h : 3 * h + 3]
                new_top = jnp.maximum(top, jnp.max(scores[h], axis=0, keepdims=True))
                weights = jnp.exp(scores[h] - new_top)
                fade = jnp.exp(top - new_top)
                total = total * fade + jnp.sum(weights, axis=0, keepdims=True)
                values = vt[HEAD_DIM * h : HEAD_DIM * (h + 1), pl.ds(koff, bk)]
                mixed = mixed * fade + dot(values, weights.astype(BF))
                out += [new_top, total, mixed]
            return tuple(out)

        start = (
            jnp.full((1, bq), -3e38, F32),
            jnp.zeros((1, bq), F32),
            jnp.zeros((HEAD_DIM, bq), F32),
        )
        done = lax.fori_loop(lo_ref[i], hi_ref[i], key_block, start * 2)
        mixed = jnp.concatenate([done[2] / done[1], done[5] / done[4]], axis=0)
        o_ref[pl.ds(off, bq), :] = mixed.T.astype(BF)
        lse_ref[0, 0:1, pl.ds(off, bq)] = done[0] + jnp.log(done[1])
        lse_ref[0, 1:2, pl.ds(off, bq)] = done[3] + jnp.log(done[4])
        return 0

    lax.fori_loop(0, length // bq, query_block, 0)


def block_ranges(segment, block, other):
    first, last = segment[::block], segment[block - 1 :: block]
    low = jnp.sum(segment[None, :] < first[:, None], axis=1)
    high = jnp.sum(segment[None, :] <= last[:, None], axis=1)
    return (low // other).astype(jnp.int32), ((high + other - 1) // other).astype(jnp.int32)


def document_features(segment):
    lane = lax.broadcasted_iota(jnp.int32, (segment.shape[0], LANES), 1) % HEAD_DIM
    same = lane == segment[:, None]
    query = jnp.where(same, 1.0, 0.0).astype(BF)
    key = jnp.where((lane < 4) & ~same, MASKED, 0.0).astype(BF)
    return query, key


def attend(queries, keys, values, segment, features, bq=1024, bk=512):
    length, width = queries.shape
    bq, bk = min(bq, length), min(bk, length)
    pairs = width // LANES
    low, high = block_ranges(segment, bq, bk)
    pair = pl.BlockSpec((length, LANES), lambda p, *_: (0, p))
    fixed = pl.BlockSpec((length, LANES), lambda p, *_: (0, 0))
    scratch = pltpu.VMEM((2, length, LANES), BF)
    return pl.pallas_call(
        functools.partial(attend_kernel, bq=bq, bk=bk),
        grid_spec=pltpu.PrefetchScalarGridSpec(
            num_scalar_prefetch=2,
            grid=(pairs,),
            in_specs=[pair, pair, pair, fixed, fixed],
            out_specs=[pair, pl.BlockSpec((1, 2, length), lambda p, *_: (p, 0, 0))],
            scratch_shapes=[scratch, scratch, pltpu.VMEM((LANES, length), BF)],
        ),
        out_shape=[shape_of((length, width), BF), shape_of((pairs, 2, length), F32)],
        compiler_params=params(),
        name="attend",
    )(low, high, queries, keys, values, *features)


def attend_back_kernel(lo_ref, hi_ref, q_ref, k_ref, v_ref, do_ref, o_ref, lse_ref, fq_ref,
                       fk_ref, cos_ref, sin_ref, dq_ref, dk_ref, dv_ref,
                       qz, kz, qm, dm, vm, kt, delta, dqt, *, bq, bk):
    length = q_ref.shape[0]
    zero = jnp.zeros((length, LANES), BF)
    qz[0], qz[1] = split_heads(q_ref[...], fq_ref[...])
    kz[0], kz[1] = split_heads(k_ref[...], fk_ref[...])
    qm[0], qm[1] = split_heads(q_ref[...], zero)
    dm[0], dm[1] = split_heads(do_ref[...], zero)
    vm[0], vm[1] = split_heads(v_ref[...], zero)
    kt[...] = k_ref[...].T
    product = (do_ref[...].astype(F32) * o_ref[...].astype(F32)).T
    delta[0:1, :] = jnp.sum(product[:HEAD_DIM], axis=0, keepdims=True)
    delta[1:2, :] = jnp.sum(product[HEAD_DIM:], axis=0, keepdims=True)
    dqt[...] = jnp.zeros_like(dqt)

    def unrotate(grad, off, rows):
        cos, sin = cos_ref[pl.ds(off, rows), :], sin_ref[pl.ds(off, rows), :]
        return (grad * cos - swap_halves(grad) * sin).astype(BF)

    def key_block(j, _):
        koff = pl.multiple_of(j * bk, bk)
        keys = [kz[h, pl.ds(koff, bk), :] for h in range(2)]
        values = [vm[h, pl.ds(koff, bk), :] for h in range(2)]

        def query_block(i, carry):
            dk, dv = carry
            off = pl.multiple_of(i * bq, bq)
            scores = [dot(keys[h], qz[h, pl.ds(off, bq), :], NT) for h in range(2)]
            grads = [dot(values[h], dm[h, pl.ds(off, bq), :], NT) for h in range(2)]
            for h in range(2):
                weights = jnp.exp(scores[h] - lse_ref[0, h : h + 1, pl.ds(off, bq)])
                dv = dv + dot(weights.astype(BF), dm[h, pl.ds(off, bq), :])
                ds = (weights * (grads[h] - delta[h : h + 1, pl.ds(off, bq)])).astype(BF)
                dk = dk + dot(ds, qm[h, pl.ds(off, bq), :])
                head = slice(HEAD_DIM * h, HEAD_DIM * (h + 1))
                dqt[head, pl.ds(off, bq)] += dot(kt[head, pl.ds(koff, bk)], ds)
            return dk, dv

        zeros = jnp.zeros((bk, LANES), F32)
        dk, dv = lax.fori_loop(lo_ref[j], hi_ref[j], query_block, (zeros, zeros))
        dk_ref[pl.ds(koff, bk), :] = unrotate(dk, koff, bk)
        dv_ref[pl.ds(koff, bk), :] = dv.astype(BF)
        return 0

    lax.fori_loop(0, length // bk, key_block, 0)
    dq_ref[...] = unrotate(dqt[...].T * HEAD_DIM**-0.5, 0, length)


def attend_back(queries, keys, values, upstream, mixed, lse, segment, features, tables,
                bq=512, bk=256):
    length, width = queries.shape
    bq, bk = min(bq, length), min(bk, length)
    pairs = width // LANES
    low, high = block_ranges(segment, bk, bq)
    pair = pl.BlockSpec((length, LANES), lambda p, *_: (0, p))
    fixed = pl.BlockSpec((length, LANES), lambda p, *_: (0, 0))
    scratch = pltpu.VMEM((2, length, LANES), BF)
    return pl.pallas_call(
        functools.partial(attend_back_kernel, bq=bq, bk=bk),
        grid_spec=pltpu.PrefetchScalarGridSpec(
            num_scalar_prefetch=2,
            grid=(pairs,),
            in_specs=[pair] * 5
            + [pl.BlockSpec((1, 2, length), lambda p, *_: (p, 0, 0))]
            + [fixed] * 4,
            out_specs=[pair] * 3,
            scratch_shapes=[scratch] * 5
            + [
                pltpu.VMEM((LANES, length), BF),
                pltpu.VMEM((8, length), F32),
                pltpu.VMEM((LANES, length), F32),
            ],
        ),
        out_shape=[shape_of((length, width), BF)] * 3,
        compiler_params=params(),
        name="attend_back",
    )(low, high, queries, keys, values, upstream, mixed, lse, *features, *tables)


def middle_kernel(half, x_ref, g_ref, c_ref, o_ref, wa_ref, p_ref, woa_ref, wob_ref, w1a_in,
                  w1b_in, w2a_in, w2b_in,
                  res_ref, dx_ref, do_ref, z_ref, gy_ref, h_ref, du_ref, ga_ref, dwa_ref,
                  dp_ref, slope, w1a_ref, w1b_ref, w2a_ref, w2b_ref, sems, *, chunk):
    width = x_ref.shape[1]
    own = width // 2
    hidden = w1a_ref.shape[1]
    loads = [
        pltpu.make_async_copy(src.at[:, pl.ds(0, hidden)], dst, sems.at[index])
        for index, (src, dst) in enumerate(
            ((w1a_in, w1a_ref), (w2a_in, w2a_ref), (w1b_in, w1b_ref), (w2b_in, w2b_ref))
        )
    ]

    @pl.when(pl.program_id(0) == 0)
    def _():
        for load in loads:
            load.start()

    cond = silu_low(c_ref[...])

    def modulation(block):
        rows = wa_ref[block * width : (block + 1) * width, :]
        return dot(cond, rows, NT) + p_ref[block + 2 : block + 3, :]

    gate_one, shift, scale, gate_two = (modulation(block) for block in (2, 3, 4, 5))
    branch = dot(o_ref[:, :own], woa_ref[...], NT) + dot(o_ref[:, own:], wob_ref[...], NT)
    middle = x_ref[...].astype(F32) + gate_one * branch
    normal, rstd = normalize(middle)
    gain = p_ref[1:2, :]
    spread = 1.0 + scale
    h = (normal * gain * spread + shift).astype(BF)
    h_ref[...] = h

    @pl.when(pl.program_id(0) == 0)
    def _():
        for load in loads:
            load.wait()

    out = jnp.zeros_like(middle)
    for start, up_ref, down_ref in ((0, w1a_ref, w2a_ref), (hidden, w1b_ref, w2b_ref)):
        for at in range(0, hidden, chunk):
            u = dot(h, up_ref[:, at : at + chunk])
            square = u * u
            flat = jnp.tanh(math.sqrt(2.0 / math.pi) * u * (1.0 + 0.044715 * square))
            half_up = 0.5 * (1.0 + flat)
            z = (u * half_up).astype(BF)
            z_ref[:, start + at : start + at + chunk] = z
            slope[:, start + at : start + at + chunk] = half_up + 0.5 * u * (
                1.0 - flat * flat
            ) * (math.sqrt(2.0 / math.pi) * (1.0 + 3.0 * 0.044715 * square))
            out = out + dot(z, down_ref[:, at : at + chunk], NT)

    g = g_ref[...].astype(F32)
    res_ref[...] = (middle + gate_two * out).astype(BF)
    gy = (gate_two * g).astype(BF)
    gy_ref[...] = gy
    dgate_two = (g * out).astype(BF)

    dh = jnp.zeros_like(middle)
    for start, up_ref, down_ref in ((0, w1a_ref, w2a_ref), (hidden, w1b_ref, w2b_ref)):
        for at in range(0, hidden, chunk):
            dz = dot(gy, down_ref[:, at : at + chunk])
            du = (dz * slope[:, start + at : start + at + chunk]).astype(BF)
            du_ref[:, start + at : start + at + chunk] = du
            dh = dh + dot(du, up_ref[:, at : at + chunk], NT)

    dn = dh * normal
    dx = g + norm_backward(dh * gain * spread, normal, rstd)
    dx_ref[...] = dx
    ga = (gate_one * dx).astype(BF)
    ga_ref[...] = ga
    do_ref[:, :own] = dot(ga, woa_ref[...]).astype(BF)
    do_ref[:, own:] = dot(ga, wob_ref[...]).astype(BF)

    @pl.when(pl.program_id(0) == 0)
    def _():
        dwa_ref[...] = jnp.zeros_like(dwa_ref)
        dp_ref[...] = jnp.zeros_like(dp_ref)

    rows = cond_rows(cond)
    grads = ((dx * branch).astype(BF), dh.astype(BF), (dn * gain).astype(BF), dgate_two)
    for block, grad in enumerate(grads):
        dwa_ref[:, block * width : (block + 1) * width] += dot(rows, grad)
    dp_ref[0:1, :] += jnp.sum(dn * spread, axis=0, keepdims=True)


def middle_stage(half, tokens, out_grad, cond, mixed, wa, norms, up_near, up_far, down_near,
                 down_far):
    width = tokens.shape[1]
    rows = mixed.shape[0]
    hidden = up_near.shape[1]
    blocks = rows // ROW_BLOCK
    mine = lambda i, half: (half[0] * blocks + i, 0)
    plain = lambda i, half: (i, 0)
    row = pl.BlockSpec((ROW_BLOCK, width), plain)
    wide = pl.BlockSpec((ROW_BLOCK, 2 * hidden), plain)
    narrow = shape_of((rows, width), BF)
    broad = shape_of((rows, 2 * hidden), BF)
    total = (cond.shape[1] + 16, 4 * width)
    return pl.pallas_call(
        functools.partial(middle_kernel, chunk=768),
        grid_spec=pltpu.PrefetchScalarGridSpec(
            num_scalar_prefetch=1,
            grid=(blocks,),
            in_specs=[
                pl.BlockSpec((ROW_BLOCK, width), mine),
                pl.BlockSpec((ROW_BLOCK, width), mine),
                pl.BlockSpec((ROW_BLOCK, cond.shape[1]), mine),
                row,
                resident(wa.shape, (0, 0)),
                resident(norms.shape, (0, 0)),
                resident((width, width // 2), (0, 2 * hidden // width)),
                resident((width, width // 2), (0, 2 * hidden // width)),
                *[pl.BlockSpec(memory_space=pl.ANY)] * 4,
            ],
            out_specs=[row, row, row, wide, row, row, wide, row,
                       pl.BlockSpec(total, lambda i, half: (0, 0)),
                       pl.BlockSpec((8, width), lambda i, half: (0, 0))],
            scratch_shapes=[pltpu.VMEM((ROW_BLOCK, 2 * hidden), F32)]
            + [pltpu.VMEM((width, hidden), BF)] * 4
            + [pltpu.SemaphoreType.DMA((4,))],
        ),
        out_shape=[narrow, shape_of((rows, width), F32), narrow, broad, narrow, narrow, broad,
                   narrow, shape_of(total, F32), shape_of((8, width), F32)],
        compiler_params=params(),
        name="middle_stage",
    )(half, tokens, out_grad, cond, mixed, wa, norms, down_near, down_far, up_near, up_far,
      down_near, down_far)


def last_kernel(half, x_ref, c_ref, dx_ref, dq_ref, dk_ref, dv_ref, wa_ref, p_ref, wqa_ref,
                wqb_ref, out_ref, dwa_ref, dp_ref):
    width = x_ref.shape[1]
    own = width // 2
    cond = silu_low(c_ref[...])
    scale = dot(cond, wa_ref[width : 2 * width, :], NT) + p_ref[3:4, :]
    dh = jnp.zeros(x_ref.shape, F32)
    for start, w_ref in ((0, wqa_ref), (own, wqb_ref)):
        cols = slice(start, start + own)
        for index, grad_ref in enumerate((dq_ref, dk_ref, dv_ref)):
            dh = dh + dot(grad_ref[:, cols], w_ref[:, index * own : (index + 1) * own], NT)
    normal, rstd = normalize(x_ref[...].astype(F32))
    gain = p_ref[0:1, :]
    spread = 1.0 + scale
    dn = dh * normal
    out_ref[...] = dx_ref[...] + norm_backward(dh * gain * spread, normal, rstd)

    @pl.when(pl.program_id(0) == 0)
    def _():
        dwa_ref[...] = jnp.zeros_like(dwa_ref)
        dp_ref[...] = jnp.zeros_like(dp_ref)

    rows = cond_rows(cond)
    dwa_ref[:, :width] += dot(rows, dh.astype(BF))
    dwa_ref[:, width:] += dot(rows, (dn * gain).astype(BF))
    dp_ref[0:1, :] += jnp.sum(dn * spread, axis=0, keepdims=True)


def last_stage(half, tokens, cond, dx, grads, wa, norms, near, far):
    width = tokens.shape[1]
    rows = dx.shape[0]
    blocks = rows // ROW_BLOCK
    mine = lambda i, half: (half[0] * blocks + i, 0)
    row = pl.BlockSpec((ROW_BLOCK, width), lambda i, half: (i, 0))
    total = (cond.shape[1] + 16, 2 * width)
    return pl.pallas_call(
        last_kernel,
        grid_spec=pltpu.PrefetchScalarGridSpec(
            num_scalar_prefetch=1,
            grid=(blocks,),
            in_specs=[
                pl.BlockSpec((ROW_BLOCK, width), mine),
                pl.BlockSpec((ROW_BLOCK, cond.shape[1]), mine),
                row, row, row, row,
                resident(wa.shape, (0, 0)),
                resident(norms.shape, (0, 0)),
                resident((width, 3 * width // 2), (0, 0)),
                resident((width, 3 * width // 2), (0, 0)),
            ],
            out_specs=[row, pl.BlockSpec(total, lambda i, half: (0, 0)),
                       pl.BlockSpec((8, width), lambda i, half: (0, 0))],
        ),
        out_shape=[shape_of((rows, width), F32), shape_of(total, F32), shape_of((8, width), F32)],
        compiler_params=params(),
        name="last_stage",
    )(half, tokens, cond, dx, *grads, wa, norms, near, far)


def weight_grad_kernel(*refs, plan):
    lefts, rights = plan["lefts"], plan["rights"]
    left_refs, right_refs = refs[:lefts], refs[lefts : lefts + rights]
    out_ref, turned = refs[lefts + rights :]
    step = pl.program_id(0)
    for begin, end, left, right in plan["spans"]:

        @pl.when(step == begin)
        def _():
            turned[...] = left_refs[left][...].T

        @pl.when((step >= begin) & (step < end))
        def _():
            out_ref[...] = dot(turned[...], right_refs[right][...]).astype(BF)


def weight_grads(lefts, rights, spans, block, name):
    rows, width = lefts[0].shape
    begin, plan, maps = 0, [], []
    for steps, left, right, first in spans:
        plan.append((begin, begin + steps, left, right))
        maps.append((begin, steps, first))
        begin += steps

    def column_map(begin, steps, first):
        return lambda i: (0, first + jnp.clip(i - begin, 0, steps - 1))

    return pl.pallas_call(
        functools.partial(
            weight_grad_kernel,
            plan={"lefts": len(lefts), "rights": len(rights), "spans": plan},
        ),
        grid=(begin,),
        in_specs=[resident((rows, width), (0, 0))] * len(lefts)
        + [pl.BlockSpec((rows, block), column_map(*entry)) for entry in maps],
        out_specs=pl.BlockSpec((width, block), lambda i: (0, i)),
        out_shape=shape_of((width, begin * block), BF),
        scratch_shapes=[pltpu.VMEM((width, rows), BF)],
        compiler_params=params(),
        name=name,
    )(*lefts, *rights)


class Gather:
    def __init__(self, shard, near, far, cut, sems, place, inner_first=False):
        outer, x, y, z, core = (place[name] for name in ("outer", "x", "y", "z", "core"))
        columns = near.shape[-1]
        flat = len(near.shape) == 2
        rows = near.shape[0] // (4 * outer)

        def slots(ref, first, number, cols):
            if flat:
                at = pl.multiple_of(first * rows, 16)
                return ref.at[pl.ds(at, number * rows), cols]
            return ref.at[pl.ds(first, number), core, :, cols]

        self.count = 0

        def copy(src, dst, device):
            index = self.count
            self.count += 1
            return pltpu.make_async_remote_copy(
                src_ref=src,
                dst_ref=dst,
                send_sem=sems.at[0, index],
                recv_sem=sems.at[1, index],
                device_id=device,
                device_id_type=pl.DeviceIdType.MESH,
            )

        here = 2 * y + x
        across_x = (4 * z + 2 * y + 1 - x, core)
        across_y = (4 * z + 2 * (1 - y) + x, core)
        other_core = (4 * z + here, 1 - core)
        whole = slice(None)
        self.outer = outer
        own = slots(near, 4 * z + here, 1, whole)
        self.local = (shard, own)
        self.inner_first = inner_first
        beyond = [(4 * lax.rem(z + hop, outer) + here, core) for hop in range(1, outer)]
        self.hops = [[copy(shard, own, device)] for device in beyond if not inner_first]
        self.one, self.two, self.swap = [], [], []
        for step in range(outer):
            base = 4 * lax.rem(z + outer - step, outer)
            one, two = [], []
            for odd, cols in enumerate((slice(0, cut), slice(cut, columns))):
                if odd and cut == columns:
                    continue
                mine = slots(near, base + here, 1, cols)
                src = mine
                if step == 0:
                    src = shard.at[:, cols] if flat else shard.at[:, :, cols]
                if step == 0 or not inner_first:
                    one.append(copy(src, mine, across_y if odd else across_x))
                if odd:
                    both = [slots(near, base + 2 * yy + x, 1, cols) for yy in range(2)]
                else:
                    both = [slots(near, base + 2 * y, 2, cols)]
                two += [copy(spot, spot, across_x if odd else across_y) for spot in both]
            self.one.append(one)
            self.two.append(two)
            if step == 0 and inner_first:
                spots = [slots(near, base + 2 * y, 2, slice(0, cut))]
                spots += [slots(near, base + 2 * yy + x, 1, slice(cut, columns)) for yy in range(2)]
                self.hops = [[copy(spot, spot, device) for spot in spots] for device in beyond]
            target = far if flat else near
            self.swap.append(
                [copy(slots(near, base, 4, whole), slots(target, base, 4, whole), other_core)]
            )

    @staticmethod
    def semaphores(outer):
        return pltpu.SemaphoreType.DMA((2, 8 * outer))

    @staticmethod
    def begin(copies):
        for entry in copies:
            entry.start()

    @staticmethod
    def arrive(copies):
        for entry in copies:
            entry.wait_recv()

    def start_hops(self):
        if self.inner_first:
            self.arrive(self.one[0])
        for entry in self.hops:
            self.begin(entry)

    def phase_one(self, step):
        if step:
            self.arrive(self.hops[step - 1])
        self.begin(self.one[step])

    def phase_two(self, step):
        if self.inner_first:
            if step:
                self.arrive(self.hops[step - 1])
        else:
            self.arrive(self.one[step])
        self.begin(self.two[step])

    def phase_swap(self, step):
        self.arrive(self.two[step])
        self.begin(self.swap[step])

    def finish(self, step):
        self.arrive(self.swap[step])

    def drain(self):
        for copies in self.hops + self.one + self.two + self.swap:
            for entry in copies:
                entry.wait_send()


def my_place(count):
    me, core = lax.axis_index("dp"), lax.axis_index("mp")
    return {"outer": count // 4, "z": me // 4, "y": lax.rem(me // 2, 2), "x": lax.rem(me, 2),
            "core": core, "me": me}


def greet(devices):
    barrier = pltpu.get_barrier_semaphore()
    for device in devices:
        pl.semaphore_signal(barrier, inc=1, device_id=device, device_id_type=pl.DeviceIdType.MESH)


def meet(devices):
    pl.semaphore_wait(pltpu.get_barrier_semaphore(), len(devices))


def partners(place):
    z, y, x, core, outer = (place[name] for name in ("z", "y", "x", "core", "outer"))
    here = 2 * y + x
    others = [(4 * lax.rem(z + hop, outer) + here, core) for hop in range(1, outer)]
    return others + [(4 * z + 2 * y + 1 - x, core), (4 * z + 2 * (1 - y) + x, core),
                     (4 * z + here, 1 - core)]


def opening_kernel(tok_ref, cond_ref, seg_ref, cosa_ref, sina_ref, cosb_ref, sinb_ref, ada_ref, norm_ref, qkv_ref, out_ref,
                   up_ref, down_ref,
                   h_out, q_out, k_out, v_out, o_out, near_out, far_out, wa_out, cos_out, sin_out,
                   fq_out, fk_out, up_near, up_far, down_near, down_far, lse_ref, table_ref,
                   h_ref, q_ref, k_ref, v_ref, o_ref, near_ref, far_ref, wa_ref, cos_ref, sin_ref,
                   fq_ref, fk_ref,
                   ada_vm, small_vm, up_vm, down_vm, x_vm, c_vm, qz, kz, vt, local, saved,
                   ada_sems, small_sems, up_sems, down_sems, *, count, cuts, bk):
    place = my_place(count)
    others = partners(place)
    greet(others)
    outer, core = place["outer"], place["core"]
    rows, width = x_vm.shape
    own = width // 2
    hidden = up_ref.shape[1]
    part = width // count
    small = Gather(small_vm, near_ref, far_ref, cuts[0], small_sems, place)
    ada = Gather(ada_vm.at[pl.ds(core, 1)], wa_ref, None, ada_vm.shape[2], ada_sems, place)
    ups = Gather(up_vm, up_near, up_far, cuts[1], up_sems, place)
    downs = Gather(down_vm, down_near, down_far, cuts[2], down_sems, place, inner_first=True)

    start = pl.multiple_of(core * rows, rows)
    loads = [
        pltpu.make_async_copy(tok_ref.at[pl.ds(start, rows)], x_vm, local.at[0]),
        pltpu.make_async_copy(cond_ref.at[pl.ds(start, rows)], c_vm, local.at[1]),
    ]
    stores = [
        pltpu.make_async_copy(*entry.local, local.at[2 + index])
        for index, entry in enumerate((ada, small, ups, downs))
    ]
    saves = {
        name: pltpu.make_async_copy(src, dst, saved.at[index])
        for index, (name, src, dst) in enumerate((
            ("h", h_ref, h_out), ("q", q_ref, q_out), ("k", k_ref, k_out), ("v", v_ref, v_out),
            ("near", near_ref, near_out), ("far", far_ref, far_out), ("wa", wa_ref, wa_out),
            ("cos", cos_ref, cos_out), ("sin", sin_ref, sin_out), ("fq", fq_ref, fq_out),
            ("fk", fk_ref, fk_out),
        ))
    }
    for load in loads:
        load.start()
    ada_vm[...] = ada_ref[...].astype(BF).reshape(ada_vm.shape)
    for c in range(3):
        small_vm[:, c * own : (c + 1) * own] = qkv_ref[c].astype(BF)
    spare = jnp.zeros((LANES - 8, part), F32)
    small_vm[:, 3 * own :] = jnp.concatenate([norm_ref[...], spare], axis=0).T.astype(BF)
    up_vm[...] = up_ref[...].astype(BF)
    down_vm[:, :hidden] = down_ref[...].astype(BF)
    down_vm[:, hidden:] = out_ref[...].astype(BF)
    meet(others)
    first = (ada, small)

    def each(method, *args):
        for entry in first:
            getattr(entry, method)(*args)

    each("start_hops")
    each("phase_one", 0)
    stores[0].start()
    stores[1].start()
    stores[2].start()
    stores[3].start()
    stores[0].wait()
    stores[1].wait()
    each("phase_two", 0)
    downs.phase_one(0)
    each("phase_one", 1)
    fine = cosb_ref.shape[0]
    for step in range(cosa_ref.shape[0]):
        at, row = slice(step * fine, (step + 1) * fine), slice(step, step + 1)
        cos_ref[at, :] = cosa_ref[row, :] * cosb_ref[...] - sina_ref[row, :] * sinb_ref[...]
        sin_ref[at, :] = sina_ref[row, :] * cosb_ref[...] + cosa_ref[row, :] * sinb_ref[...]
    each("phase_one", 2)
    each("phase_two", 1)
    documents = seg_ref[pl.ds(core, 1), :].astype(F32)
    documents = jnp.broadcast_to(documents, (LANES, rows)).T
    lane = (lax.broadcasted_iota(jnp.int32, (rows, LANES), 1) % HEAD_DIM).astype(F32)
    same = documents == lane
    fq_ref[...] = jnp.where(same, 1.0, 0.0).astype(BF)
    fk_ref[...] = jnp.where(same, 0.0, jnp.where(lane < 4.0, MASKED, 0.0)).astype(BF)
    each("phase_one", 3)
    ups.start_hops()
    each("phase_two", 2)
    stores[2].wait()
    stores[3].wait()
    downs.start_hops()
    each("phase_two", 3)
    ups.phase_one(0)
    for load in loads:
        load.wait()
    for name in ("cos", "sin", "fq", "fk"):
        saves[name].start()
    for step in range(2):
        each("phase_swap", step)
    ups.phase_two(0)
    ups.phase_one(1)
    downs.phase_two(0)
    for step in range(2, outer):
        each("phase_swap", step)
    for step in range(outer):
        each("finish", step)
    for name in ("near", "far", "wa"):
        saves[name].start()

    table_ref[...] = near_ref[:, 3 * own :].astype(F32).T[0:8, :]
    wa = wa_ref[...].reshape(6 * width, c_vm.shape[1])

    def wide_events(tick):
        if tick == 0:
            ups.phase_two(1)
            ups.phase_one(2)
        if tick == 2:
            ups.phase_one(3)
            ups.phase_two(2)
        if tick == 4:
            ups.phase_two(3)
            downs.phase_two(1)
            ups.phase_swap(0)
        if tick == 6:
            downs.phase_two(2)
            downs.phase_swap(0)
            ups.phase_swap(1)
        if tick == 7:
            ups.phase_swap(2)
            downs.phase_swap(1)
        if tick == 8:
            ups.phase_swap(3)

    def row_block(i, _):
        at = pl.ds(pl.multiple_of(i * ROW_BLOCK, ROW_BLOCK), ROW_BLOCK)
        cond = silu_low(c_vm[at, :])
        shift = dot(cond, wa[:width], NT) + table_ref[2:3, :]
        scale = dot(cond, wa[width : 2 * width], NT) + table_ref[3:4, :]
        normal, _ = normalize(x_vm[at, :].astype(F32))
        h = (normal * table_ref[0:1, :] * (1.0 + scale) + shift).astype(BF)
        h_ref[at, :] = h
        cos = jnp.concatenate([cos_ref[at, :]] * (own // LANES), axis=1)
        sin = jnp.concatenate([sin_ref[at, :]] * (own // LANES), axis=1)
        for first, w_ref in ((0, near_ref), (own, far_ref)):
            cols = slice(first, first + own)
            query = dot(h, w_ref[:, 0:own])
            query = query * cos + swap_halves(query) * sin
            q_ref[at, cols] = (query * HEAD_DIM**-0.5).astype(BF)
            key = dot(h, w_ref[:, own : 2 * own])
            k_ref[at, cols] = (key * cos + swap_halves(key) * sin).astype(BF)
            v_ref[at, cols] = dot(h, w_ref[:, 2 * own : 3 * own]).astype(BF)
        for tick in range(4):

            @pl.when(i == tick)
            def _():
                wide_events(tick)

        return 0

    lax.fori_loop(0, rows // ROW_BLOCK, row_block, 0)
    for name in ("h", "q", "k", "v"):
        saves[name].start()

    def keep(p):
        lanes = pl.ds(pl.multiple_of(p * LANES, LANES), LANES)
        return pltpu.make_async_copy(o_ref.at[:, lanes], o_out.at[:, lanes], saved.at[len(saves)])

    def head_pair(p, _):
        lanes = pl.ds(pl.multiple_of(p * LANES, LANES), LANES)
        qz[0], qz[1] = split_heads(q_ref[:, lanes], fq_ref[...])
        kz[0], kz[1] = split_heads(k_ref[:, lanes], fk_ref[...])
        vt[...] = v_ref[:, lanes].T
        state = [None, None]
        for j in range(rows // bk):
            block = slice(j * bk, (j + 1) * bk)
            scores = [dot(kz[h, block, :], qz[h], NT) for h in range(2)]
            for h in range(2):
                values = vt[HEAD_DIM * h : HEAD_DIM * (h + 1), block]
                top = jnp.max(scores[h], axis=0, keepdims=True)
                if j:
                    top = jnp.maximum(state[h][0], top)
                weights = jnp.exp(scores[h] - top)
                total = jnp.sum(weights, axis=0, keepdims=True)
                result = dot(values, weights.astype(BF))
                if j:
                    fade = jnp.exp(state[h][0] - top)
                    total = state[h][1] * fade + total
                    result = state[h][2] * fade + result
                state[h] = (top, total, result)
        done = jnp.concatenate([entry[2] / entry[1] for entry in state], axis=0)
        o_ref[:, lanes] = done.T.astype(BF)
        for h in range(2):
            lse_ref[p, h : h + 1, :] = state[h][0] + jnp.log(state[h][1])

        @pl.when(p > 0)
        def _():
            keep(p - 1).wait()

        keep(p).start()
        for tick in range(4, 10):

            @pl.when(p == tick - 4)
            def _():
                wide_events(tick)

        return 0

    lax.fori_loop(0, width // LANES, head_pair, 0)
    downs.phase_two(3)
    downs.phase_swap(2)
    downs.phase_swap(3)
    keep(width // LANES - 1).wait()
    for save in saves.values():
        save.wait()
    for step in range(outer):
        ups.finish(step)
        downs.finish(step)
    for entry in (ada, small, ups, downs):
        entry.drain()


def opening(count, tokens, cond, segments, rope, weights):
    ada, norms, qkv, out, up, down = weights
    rows, width = tokens.shape[0] // 2, tokens.shape[1]
    conds, part, hidden = cond.shape[1], width // count, up.shape[1]
    vm = pl.BlockSpec(memory_space=pltpu.VMEM)
    hbm = pl.BlockSpec(memory_space=pl.ANY)
    small = shape_of((width, 3 * width // 2 + LANES), BF)
    act = shape_of((rows, width), BF)
    table = shape_of((rows, LANES), F32)
    feature = shape_of((rows, LANES), BF)
    first = shape_of((width, hidden), BF)
    second = shape_of((width, hidden + width // 2), BF)
    pairs = width // LANES
    pair = pltpu.VMEM((2, rows, LANES), BF)
    half_cols = ada.shape[0] // 2
    kept = [act] * 5 + [small, small, shape_of((count, 2, half_cols, conds), BF), table, table,
                        feature, feature]
    cuts = (512, hidden // 2, second.shape[1] // 2 // LANES * LANES)
    return pl.pallas_call(
        functools.partial(opening_kernel, count=count, cuts=cuts, bk=512),
        in_specs=[hbm, hbm] + [vm] * 11,
        out_specs=[hbm] * (len(kept) + 4) + [vm, vm],
        out_shape=kept + [first, first, second, second]
        + [shape_of((pairs, 2, rows), F32), shape_of((8, width), F32)],
        scratch_shapes=[pltpu.VMEM(entry.shape, entry.dtype) for entry in kept]
        + [
            pltpu.VMEM((2, half_cols, conds), BF),
            pltpu.VMEM((part, small.shape[1]), BF),
            pltpu.VMEM((part, hidden), BF),
            pltpu.VMEM((part, second.shape[1]), BF),
            pltpu.VMEM((rows, width), BF), pltpu.VMEM((rows, conds), BF),
            pair, pair, pltpu.VMEM((LANES, rows), BF),
            pltpu.SemaphoreType.DMA((6,)),
            pltpu.SemaphoreType.DMA((len(kept),)),
        ] + [Gather.semaphores(count // 4)] * 4,
        compiler_params=pltpu.CompilerParams(
            vmem_limit_bytes=VMEM_LIMIT, collective_id=0, has_side_effects=True
        ),
        name="opening",
    )(tokens, cond, segments, *rope, ada, norms, qkv, out, up, down)


class Scatter:
    def __init__(self, place, first, total, one, two, hops, sems):
        z, y, x, core, outer = (place[name] for name in ("z", "y", "x", "core", "outer"))

        def copy(src, dst, device):
            index = place["next"]
            place["next"] = index + 1
            return pltpu.make_async_remote_copy(
                src_ref=src,
                dst_ref=dst,
                send_sem=sems.at[0, index],
                recv_sem=sems.at[1, index],
                device_id=device,
                device_id_type=pl.DeviceIdType.MESH,
            )

        across_x = (4 * z + 2 * y + 1 - x, core)
        across_y = (4 * z + 2 * (1 - y) + x, core)
        self.one, self.two, self.hops, self.z, self.outer = one, two, hops, z, outer
        if first == "y":
            self.keep_one, self.keep_two = total.at[:, y], one.at[:, x]
            self.copy_one = copy(total.at[:, 1 - y], one, across_y)
            self.copy_two = copy(one.at[:, 1 - x], two, across_x)
        else:
            self.keep_one, self.keep_two = total.at[:, :, x], one.at[:, y]
            self.copy_one = copy(total.at[:, :, 1 - x], one, across_x)
            self.copy_two = copy(one.at[:, 1 - y], two, across_y)
        self.copy_hops = [
            copy(two.at[lax.rem(z + hop, outer)], hops.at[hop - 1],
                 (4 * lax.rem(z + hop, outer) + 2 * y + x, core))
            for hop in range(1, outer)
        ]

    @classmethod
    def halves(cls, place, buffers, sems, order="yx"):
        columns = buffers[0].shape[-1]
        cut = columns // 2 // LANES * LANES
        out = []
        for first, cols in zip(order, (slice(0, cut), slice(cut, columns))):
            views = [ref.at[(slice(None),) * (len(ref.shape) - 1) + (cols,)] for ref in buffers]
            out.append(cls(place, first, *views, sems))
        return out

    def start(self):
        self.copy_one.start()

    def phase_two(self):
        self.copy_one.wait_recv()
        self.one[...] = self.one[...] + self.keep_one[...]
        self.copy_two.start()

    def phase_hops(self):
        self.copy_two.wait_recv()
        self.two[...] = self.two[...] + self.keep_two[...]
        for entry in self.copy_hops:
            entry.start()

    def finish(self):
        total = self.two[self.z].astype(F32)
        for hop, entry in enumerate(self.copy_hops):
            entry.wait_recv()
            total = total + self.hops[hop].astype(F32)
        return total

    def drain(self):
        for entry in [self.copy_one, self.copy_two] + self.copy_hops:
            entry.wait_send()


def across_cores(place, src, dst, sems):
    index = place["next"]
    place["next"] = index + 1
    return pltpu.make_async_remote_copy(
        src_ref=src,
        dst_ref=dst,
        send_sem=sems.at[0, index],
        recv_sem=sems.at[1, index],
        device_id=(place["me"], 1 - place["core"]),
        device_id_type=pl.DeviceIdType.MESH,
    )


def scatter_buffers(outer, blocks, rows, columns):
    lead = () if blocks is None else (blocks,)
    return [
        pltpu.VMEM(lead + (outer, 2, 2, rows, columns), BF),
        pltpu.VMEM(lead + (outer, 2, 2, rows, columns), BF),
        pltpu.VMEM(lead + (outer, 2, rows, columns), BF),
        pltpu.VMEM(lead + (outer, rows, columns), BF),
        pltpu.VMEM(lead + (outer - 1, rows, columns), BF),
    ]


def spread_kernel(h_in, gy_in, ga_in, du_ref, z_ref, o_in, q_in, k_in, v_in, do_in, lse_in,
                  fq_in, fk_in, cos_in, sin_in,
                  dq_out, dk_out, dv_out, last_ref, sum_ref,
                  h_ref, gy_ref, ga_ref, o_ref, q_ref, k_ref, v_ref, do_ref, lse_ref,
                  fq_ref, fk_ref, cos_ref, sin_ref, dq_ref, dk_ref, dv_ref,
                  h_turn, gy_turn, ga_turn, right, far6, sum6, one6, two6, hop6, far1,
                  qz, kz, qm, dm, vm, kt, delta, dqt,
                  load_sems, input_sems, keep_sems, sems, *, count, bk):
    place = my_place(count)
    others = partners(place)
    greet(others)
    place["next"] = 0
    outer = place["outer"]
    rows, width = o_ref.shape
    pieces = (
        (h_in, h_ref), (gy_in, gy_ref), (ga_in, ga_ref), (o_in, o_ref), (q_in, q_ref),
        (k_in, k_ref), (v_in, v_ref), (do_in, do_ref), (lse_in, lse_ref), (fq_in, fq_ref),
        (fk_in, fk_ref), (cos_in, cos_ref), (sin_in, sin_ref),
    )
    inputs = [
        pltpu.make_async_copy(src, dst, input_sems.at[index])
        for index, (src, dst) in enumerate(pieces)
    ]
    own = width // 2
    each, block = right.shape[0], right.shape[2]
    span = 2 * each * block
    shards = far6.shape[1:]
    tail = far1.shape

    swaps = [across_cores(place, far6.at[j], sum6.at[j], sems) for j in range(2 * each)]
    swaps.append(across_cores(place, far1, last_ref, sems))
    scatters = [
        Scatter.halves(place, [ref.at[j] for ref in (sum6, one6, two6, hop6)], sems)
        for j in range(2 * each)
    ]

    def start(j):
        for entry in scatters[j]:
            entry.start()

    def phase_two(j):
        for entry in scatters[j]:
            entry.phase_two()

    def phase_hops(j):
        for entry in scatters[j]:
            entry.phase_hops()

    def finish(j):
        at = j * block
        for entry in scatters[j]:
            columns = entry.hops.shape[-1]
            sum_ref[:, at : at + columns] = entry.finish()
            at += columns

    lefts, sources = (h_turn, gy_turn), (du_ref, z_ref)
    groups = [(side, index) for index in range(2) for side in (1, 0)]

    def load(group, b):
        side, index = groups[group]
        at = pl.multiple_of(side * (span // 2) + b * block, block)
        return pltpu.make_async_copy(
            sources[index].at[:, pl.ds(at, block)], right.at[b], load_sems.at[b]
        )

    inputs[0].start()
    load(0, 0).start()
    for item in inputs[1:4]:
        item.start()
    for b in range(1, each):
        load(0, b).start()
    for item in inputs[4:]:
        item.start()
    inputs[0].wait()
    h_turn[...] = h_ref[...].T
    meet(others)

    for group, (side, index) in enumerate(groups):

        def grad_block(b, _):
            load(group, b).wait()
            grad = dot(lefts[index][...], right[b])
            if group + 1 < len(groups):
                load(group + 1, b).start()
            j = index * each + b
            if side:
                far6[j] = grad.reshape(shards).astype(BF)
            for b_static in range(each):
                at = index * each + b_static

                @pl.when(b == b_static)
                def _():
                    if side:
                        swaps[at].start()
                    else:
                        swaps[at].wait_recv()

            if not side:
                sum6[j] = (grad.reshape(shards) + sum6[j].astype(F32)).astype(BF)
                if index == 0:
                    for b_static in range(2):

                        @pl.when(b == b_static)
                        def _():
                            start(b_static)

            return 0

        if index == 1 and side:
            inputs[1].wait()
            gy_turn[...] = gy_ref[...].T
        lax.fori_loop(0, each, grad_block, 0)
        if index == 1 and side:
            inputs[2].wait()
            inputs[3].wait()
            ga_turn[...] = ga_ref[...].T
            grad = dot(ga_turn[...], o_ref[:, own:])
            far1[...] = grad.reshape(tail).astype(BF)
            swaps[-1].start()
            phase_two(0)
            start(2)
    grad = dot(ga_turn[...], o_ref[:, :own])
    swaps[-1].wait_recv()
    last_ref[...] = (grad.reshape(tail) + last_ref[...].astype(F32)).astype(BF)
    phase_two(1)
    start(3)
    for item in inputs[4:]:
        item.wait()

    def events(p):
        if p < 4:
            phase_two(p + 2)
        if p < 2:
            start(p + 4)
        if p < 5:
            phase_hops(p)
        if p == 4:
            phase_hops(5)
        if 1 < p:
            finish(p - 2)
        if p == 5:
            finish(4)
            finish(5)

    def keep(p):
        lanes = pl.ds(pl.multiple_of(p * LANES, LANES), LANES)
        return [
            pltpu.make_async_copy(src.at[:, lanes], dst.at[:, lanes], keep_sems.at[index])
            for index, (src, dst) in enumerate(
                ((dq_ref, dq_out), (dk_ref, dk_out), (dv_ref, dv_out))
            )
        ]

    zero = jnp.zeros((rows, LANES), BF)

    def unrotate(grad, at):
        return (grad * cos_ref[at, :] - swap_halves(grad) * sin_ref[at, :]).astype(BF)

    def head_pair(p, _):
        lanes = pl.ds(pl.multiple_of(p * LANES, LANES), LANES)
        qz[0], qz[1] = split_heads(q_ref[:, lanes], fq_ref[...])
        kz[0], kz[1] = split_heads(k_ref[:, lanes], fk_ref[...])
        qm[0], qm[1] = split_heads(q_ref[:, lanes], zero)
        dm[0], dm[1] = split_heads(do_ref[:, lanes], zero)
        vm[0], vm[1] = split_heads(v_ref[:, lanes], zero)
        kt[...] = k_ref[:, lanes].T
        product = (do_ref[:, lanes].astype(F32) * o_ref[:, lanes].astype(F32)).T
        delta[0:1, :] = jnp.sum(product[:HEAD_DIM], axis=0, keepdims=True)
        delta[1:2, :] = jnp.sum(product[HEAD_DIM:], axis=0, keepdims=True)
        dqt[...] = jnp.zeros_like(dqt)

        def key_block(j, reach):
            at = pl.ds(pl.multiple_of(j * bk, bk), bk)
            dk = jnp.zeros((bk, LANES), F32)
            dv = jnp.zeros((bk, LANES), F32)
            scores = [dot(kz[h, at, :], qz[h, reach, :], NT) for h in range(2)]
            grads = [dot(vm[h, at, :], dm[h, reach, :], NT) for h in range(2)]
            for h in range(2):
                weights = jnp.exp(scores[h] - lse_ref[p, h : h + 1, reach])
                dv = dv + dot(weights.astype(BF), dm[h, reach, :])
                ds = (weights * (grads[h] - delta[h : h + 1, reach])).astype(BF)
                dk = dk + dot(ds, qm[h, reach, :])
                head = slice(HEAD_DIM * h, HEAD_DIM * (h + 1))
                dqt[head, reach] += dot(kt[head, at], ds)
            dk_ref[at, lanes] = unrotate(dk, at)
            dv_ref[at, lanes] = dv.astype(BF)

        reaches = {}
        for first in range(0, rows, bk):
            low = max(0, (first - rows // 2 + 1) // LANES * LANES)
            high = min(rows, -(-(first + bk + rows // 2 - 1) // LANES) * LANES)
            reaches.setdefault((low, high), []).append(first // bk)
        for (low, high), blocks in reaches.items():

            def one_block(j, _):
                key_block(j, slice(low, high))
                return 0

            if len(blocks) == 1:
                key_block(blocks[0], slice(low, high))
            else:
                lax.fori_loop(blocks[0], blocks[-1] + 1, one_block, 0)

        dq_ref[:, lanes] = unrotate(dqt[...].T * HEAD_DIM**-0.5, pl.ds(0, rows))

        @pl.when(p > 0)
        def _():
            for entry in keep(p - 1):
                entry.wait()

        for entry in keep(p):
            entry.start()
        for step in range(6):

            @pl.when(p == step)
            def _():
                events(step)

        return 0

    lax.fori_loop(0, width // LANES, head_pair, 0)
    for entry in keep(width // LANES - 1):
        entry.wait()
    for entry in swaps:
        entry.wait_send()
    for pair in scatters:
        for entry in pair:
            entry.drain()


def spread(count, h_two, gy, ga, du, z, mixed, queries, keys, values, upstream, lse, features,
           tables):
    rows, width = mixed.shape
    part = width // count
    outer = count // 4
    hidden = du.shape[1] // 2
    each = 3
    block = hidden // each
    vm = pl.BlockSpec(memory_space=pltpu.VMEM)
    hbm = pl.BlockSpec(memory_space=pl.ANY)
    act = shape_of((rows, width), BF)
    last = shape_of((outer, 2, 2, part, width // 2), BF)
    turn = pltpu.VMEM((width, rows), BF)
    pair = pltpu.VMEM((2, rows, LANES), BF)
    copies = 7 + 12 * (2 + outer - 1)
    held = [h_two, gy, ga, mixed, queries, keys, values, upstream, lse, *features, *tables]
    return pl.pallas_call(
        functools.partial(spread_kernel, count=count, bk=256),
        in_specs=[hbm] * (len(held) + 2),
        out_specs=[hbm] * 3 + [vm] * 2,
        out_shape=[act, act, act, last, shape_of((part, 2 * hidden), F32)],
        scratch_shapes=[pltpu.VMEM(entry.shape, entry.dtype) for entry in held + [act] * 3]
        + [turn, turn, turn, pltpu.VMEM((each, rows, block), BF)]
        + scatter_buffers(outer, 2 * each, part, block)
        + [pltpu.VMEM(last.shape, BF)]
        + [pair] * 5
        + [
            pltpu.VMEM((LANES, rows), BF),
            pltpu.VMEM((8, rows), F32),
            pltpu.VMEM((LANES, rows), F32),
            pltpu.SemaphoreType.DMA((each,)),
            pltpu.SemaphoreType.DMA((len(held),)),
            pltpu.SemaphoreType.DMA((3,)),
            pltpu.SemaphoreType.DMA((2, copies)),
        ],
        compiler_params=pltpu.CompilerParams(
            vmem_limit_bytes=VMEM_LIMIT, collective_id=1, has_side_effects=True
        ),
        name="spread",
    )(h_two, gy, ga, du, z, mixed, queries, keys, values, upstream, lse, *features, *tables)


def closing_kernel(tok_ref, cond_ref, h_in, dq_in, dk_in, dv_in, near_in, far_in, wa_in,
                   dwa_two_in, dx_in, last_in, mid_ref, p_ref, dp_two_ref,
                   rows_ref, qkv_ref, out_ref, ada_ref, norm_ref, square_ref,
                   h_ref, grads, x_vm, c_vm, near_ref, far_ref, wa_ref, dwa_two_ref, dx_ref,
                   turned, mine, dh_vm, dwa_vm, dp_vm, dwt, plane, column,
                   far3, sum3, one3, two3, hop3, sum2, one2, two2, hop2,
                   sum1, one1, two1, hop1, local, sems, *, count, token_total):
    place = my_place(count)
    place["next"] = 0
    z, y, x, core, outer, me = (place[name] for name in ("z", "y", "x", "core", "outer", "me"))
    rows, width = x_vm.shape
    own = width // 2
    part = width // count
    conds = c_vm.shape[1]
    half_cols = ada_ref.shape[1]
    shards = far3.shape[1:]

    start = pl.multiple_of(core * rows, rows)
    columns = near_ref.shape[1]
    pieces = (
        (h_in, h_ref), (dq_in, grads.at[0]), (dk_in, grads.at[1]), (dv_in, grads.at[2]),
        (tok_ref.at[pl.ds(start, rows)], x_vm), (cond_ref.at[pl.ds(start, rows)], c_vm),
        (near_in.at[:, pl.ds(0, columns)], near_ref), (far_in.at[:, pl.ds(0, columns)], far_ref),
        (wa_in.at[pl.ds(width, width)], wa_ref), (dwa_two_in, dwa_two_ref), (dx_in, dx_ref),
        (last_in, sum1),
    )
    loads = [
        pltpu.make_async_copy(src, dst, local.at[index])
        for index, (src, dst) in enumerate(pieces)
    ]
    loads[11].start()
    for load in loads[:11]:
        load.start()

    swaps = [across_cores(place, far3.at[c], sum3.at[c], sems) for c in range(3)]
    scatters = [
        Scatter.halves(place, [ref.at[c] for ref in (sum3, one3, two3, hop3)], sems,
                       "xy" if c % 2 else "yx")
        for c in range(3)
    ]
    scatters.append(Scatter.halves(place, [sum1, one1, two1, hop1], sems, "xy"))
    dwt_rows = dwt.shape[4]
    ada_swap = across_cores(place, dwt.at[:, :, :, 1 - core], sum2, sems)
    cut = dwt_rows // 2
    adas = []
    for first, at in (("x", slice(0, cut)), ("y", slice(cut, dwt_rows))):
        views = [ref.at[(slice(None),) * (len(ref.shape) - 2) + (at,)]
                 for ref in (sum2, one2, two2, hop2)]
        adas.append(Scatter(place, first, *views, sems))
    sends = []

    def copy(src, dst, device):
        index = place["next"]
        place["next"] = index + 1
        entry = pltpu.make_async_remote_copy(
            src_ref=src, dst_ref=dst, send_sem=sems.at[0, index], recv_sem=sems.at[1, index],
            device_id=device, device_id_type=pl.DeviceIdType.MESH,
        )
        sends.append(entry)
        return entry

    row_copies = []
    for i in range(rows // ROW_BLOCK):
        at = pl.ds(i * ROW_BLOCK, ROW_BLOCK)
        row_copies.append(copy(dh_vm.at[at], rows_ref.at[1, at], (me, 1 - core)))
    ada_copy = copy(ada_ref.at[core], ada_ref.at[core], (me, 1 - core))
    spot = 4 * core + 2 * y + x
    plane_copies = []
    for other in range(1, 8):
        yy, xx = lax.rem(y + other // 2, 2), lax.rem(x + other, 2)
        cc = lax.rem(core + other // 4, 2)
        plane_copies.append((4 * z + 2 * yy + xx, cc))
    beyond = [(4 * lax.rem(z + hop, outer) + 2 * y + x, core) for hop in range(1, outer)]

    others = plane_copies + beyond
    greet(others)
    plane_copies = [copy(plane.at[spot], plane.at[spot], device) for device in plane_copies]
    column_copies = [copy(column.at[z], column.at[z], device) for device in beyond]

    def all_of(c, method):
        for entry in scatters[c]:
            getattr(entry, method)()

    loads[0].wait()
    turned[...] = h_ref[...].T
    meet(others)
    loads[11].wait()
    all_of(3, "start")

    def add_near_grad(c):
        swaps[c].wait_recv()
        sum3[c] = (mine[c] + sum3[c].astype(F32)).astype(BF)
        all_of(c, "start")

    for c in range(3):
        loads[1 + c].wait()
        grad = dot(turned[...], grads[c])
        far3[c] = grad[:, own:].reshape(shards).astype(BF)
        swaps[c].start()
        mine[c] = grad[:, :own].reshape(shards)
        if c:
            add_near_grad(c - 1)
    for load in loads[4:10]:
        load.wait()

    def place_rows(start, values):
        at = 0
        while at < values.shape[0]:
            block, low = divmod(start + at, half_cols)
            high = min(half_cols, low + values.shape[0] - at)
            shard, side = divmod(block, 2)
            dwt[shard // 4, (shard // 2) % 2, shard % 2, side, low:high, :] = values[
                at : at + high - low
            ]
            at += high - low

    place_rows(2 * width, dwa_two_ref[:conds, :].T.astype(BF))
    dwa_vm[...] = jnp.zeros_like(dwa_vm)
    dp_vm[...] = jnp.zeros_like(dp_vm)
    dp_vm[1:2, :] = dp_two_ref[0:1, :]
    for block in range(4):
        dp_vm[4 + block : 5 + block, :] = dwa_two_ref[
            conds : conds + 1, block * width : (block + 1) * width
        ]
    gain = p_ref[0:1, :]

    def spread_of(at):
        scale = dot(silu_low(c_vm[at, :]), wa_ref[...], NT) + p_ref[3:4, :]
        return 1.0 + scale

    def first_pass(i, _):
        at = pl.ds(pl.multiple_of(i * ROW_BLOCK, ROW_BLOCK), ROW_BLOCK)
        dh = jnp.zeros((ROW_BLOCK, width), F32)
        for first, w_ref in ((0, near_ref), (own, far_ref)):
            cols = slice(first, first + own)
            for c in range(3):
                dh = dh + dot(grads[c, at, cols], w_ref[:, c * own : (c + 1) * own], NT)
        dh_vm[at, :] = dh
        normal, _ = normalize(x_vm[at, :].astype(F32))
        dn = dh * normal
        summed = cond_rows(silu_low(c_vm[at, :]))
        dwa_vm[:, :width] += dot(summed, dh.astype(BF))
        dwa_vm[:, width:] += dot(summed, (dn * gain).astype(BF))
        dp_vm[0:1, :] += jnp.sum(dn * spread_of(at), axis=0, keepdims=True)

        @pl.when(i == 0)
        def _():
            add_near_grad(2)
            all_of(3, "phase_two")

        @pl.when(i == 2)
        def _():
            all_of(0, "phase_two")
            all_of(3, "phase_hops")

        @pl.when(i == 3)
        def _():
            all_of(1, "phase_two")

        return 0

    lax.fori_loop(0, rows // ROW_BLOCK, first_pass, 0)

    place_rows(0, dwa_vm[:conds, :].T.astype(BF))
    for block in range(2):
        dp_vm[2 + block : 3 + block, :] = dwa_vm[
            conds : conds + 1, block * width : (block + 1) * width
        ]
    lane = lax.broadcasted_iota(jnp.int32, (16, conds), 1)
    for shard in range(count):
        gone = dp_vm[...] if shard == 0 else pltpu.roll(dp_vm[...], width - shard * part, 1)
        gone = jnp.where(lane < part, gone[:, :conds], 0.0).astype(BF)
        for side in range(2):
            dwt[shard // 4, (shard // 2) % 2, shard % 2, side, half_cols:, :] = gone
    ada_swap.start()
    all_of(0, "phase_hops")
    all_of(2, "phase_two")
    ada_swap.wait_recv()
    sum2[...] = sum2[...] + dwt[:, :, :, core]
    for entry in adas:
        entry.start()
    all_of(1, "phase_hops")
    loads[10].wait()

    def events(i):
        if i == 1:
            all_of(2, "phase_hops")
        if i == 2:
            for entry in adas:
                entry.phase_two()
        if i == 3:
            for entry in adas:
                entry.phase_hops()

    def keep(i):
        at = pl.ds(pl.multiple_of(i * ROW_BLOCK, ROW_BLOCK), ROW_BLOCK)
        return pltpu.make_async_copy(dh_vm.at[at], rows_ref.at[0, at], local.at[i])

    def second_pass(i, _):
        at = pl.ds(pl.multiple_of(i * ROW_BLOCK, ROW_BLOCK), ROW_BLOCK)
        normal, rstd = normalize(x_vm[at, :].astype(F32))
        grad = dh_vm[at, :] * gain * spread_of(at)
        dh_vm[at, :] = dx_ref[at, :] + norm_backward(grad, normal, rstd)
        keep(i).start()
        for step in range(rows // ROW_BLOCK):

            @pl.when(i == step)
            def _():
                row_copies[step].start()
                if step < 4:
                    events(step)

        return 0

    lax.fori_loop(0, rows // ROW_BLOCK, second_pass, 0)

    squares = jnp.sum((mid_ref[...] / token_total) ** 2)
    for c in range(4):
        target, at = (qkv_ref, c * own) if c < 3 else (out_ref, 0)
        for entry in scatters[c]:
            total = entry.finish()
            target[:, at : at + total.shape[1]] = total
            squares = squares + jnp.sum((total / token_total) ** 2)
            at += total.shape[1]
    first, second = adas[0].finish(), adas[1].finish()
    rest = half_cols - cut
    ada_ref[core, 0:cut, :] = first
    ada_ref[core, cut:, :] = second[:rest]
    norm_ref[...] = second[rest : rest + 8]
    ada_copy.start()
    squares = squares + jnp.sum((first / token_total) ** 2)
    squares = squares + jnp.sum((second[:rest] / token_total) ** 2)
    squares = squares + 0.5 * jnp.sum((second[rest:] / token_total) ** 2)
    plane[spot] = jnp.full((8, LANES), squares, F32)
    for entry in plane_copies:
        entry.start()
    for entry in plane_copies:
        entry.wait_recv()
    column[z] = jnp.sum(plane[...], axis=0)
    for entry in column_copies:
        entry.start()
    for entry in column_copies:
        entry.wait_recv()
    square_ref[...] = jnp.sum(column[...], axis=0)
    ada_copy.wait_recv()
    for i, entry in enumerate(row_copies):
        keep(i).wait()
        entry.wait_recv()
    for entry in swaps + [ada_swap] + sends:
        entry.wait_send()
    for entry in [part for pair in scatters for part in pair] + adas:
        entry.drain()


def closing(count, tokens, cond, h_one, grads, dx, wa, norms, near, far, dwa_two, dp_two,
            last, middle_sum, token_total):
    rows, width = dx.shape
    conds = cond.shape[1]
    part = width // count
    outer = count // 4
    half_cols = wa.shape[0] // count // 2
    vm = pl.BlockSpec(memory_space=pltpu.VMEM)
    hbm = pl.BlockSpec(memory_space=pl.ANY)
    copies = 5 + 10 * (2 + outer - 1) + rows // ROW_BLOCK + 1 + 7 + outer - 1
    act = pltpu.VMEM((rows, width), BF)
    half_weights = pltpu.VMEM((width, 3 * width // 2), BF)
    return pl.pallas_call(
        functools.partial(closing_kernel, count=count, token_total=token_total),
        in_specs=[hbm] * 12 + [vm] * 3,
        out_specs=[hbm] + [vm] * 5,
        out_shape=[
            shape_of((2, rows, width), F32),
            shape_of((part, 3 * width // 2), F32),
            shape_of((part, width // 2), F32),
            shape_of((2, half_cols, conds), F32),
            shape_of((8, conds), F32),
            shape_of((8, LANES), F32),
        ],
        scratch_shapes=[
            act, pltpu.VMEM((3, rows, width), BF), act,
            pltpu.VMEM((rows, conds), BF),
            half_weights, half_weights,
            pltpu.VMEM((width, conds), BF),
            pltpu.VMEM(dwa_two.shape, F32),
            pltpu.VMEM((rows, width), F32),
            pltpu.VMEM((width, rows), BF),
            pltpu.VMEM((3, outer, 2, 2, part, width // 2), F32),
            pltpu.VMEM((rows, width), F32),
            pltpu.VMEM((conds + 16, 2 * width), F32),
            pltpu.VMEM((16, width), F32),
            pltpu.VMEM((outer, 2, 2, 2, half_cols + 16, conds), BF),
            pltpu.VMEM((8, 8, LANES), F32),
            pltpu.VMEM((outer, 8, LANES), F32),
        ]
        + scatter_buffers(outer, 3, part, width // 2)
        + scatter_buffers(outer, None, half_cols + 16, conds)[1:]
        + scatter_buffers(outer, None, part, width // 2)[1:]
        + [pltpu.SemaphoreType.DMA((12,)), pltpu.SemaphoreType.DMA((2, copies))],
        compiler_params=pltpu.CompilerParams(
            vmem_limit_bytes=VMEM_LIMIT, collective_id=2, has_side_effects=True
        ),
        name="closing",
    )(tokens, cond, h_one, *grads, near, far, wa, dwa_two, dx, last, middle_sum, norms, dp_two)


def update_kernel(half, step, ina_ref, inb_ref, resa_ref, resb_ref, up_ref, down_ref, qkv_ref,
                  out_ref, ada_ref, norm_ref, square_ref, *refs, token_total):
    state, (grad_out, res_out, norm_out), new = refs[:18], refs[18:21], refs[21:]
    i, steps = pl.program_id(0), pl.num_programs(0)
    here = (i // (steps // 2)) == half[0]

    @pl.when(here)
    def _():
        grad_out[...] = ina_ref[0]
        res_out[...] = resa_ref[...]

    @pl.when(jnp.logical_not(here))
    def _():
        grad_out[...] = inb_ref[0]
        res_out[...] = resb_ref[...]

    grad_norm = jnp.sqrt(square_ref[0:1, :])
    norm_out[...] = grad_norm
    clip_factor = jnp.minimum(1.0, clip_limit / (grad_norm + 1e-06))[:, 0:1] / token_total
    count = jnp.full((1, LANES), step[0], jnp.int32).astype(F32)
    fix_one = (1.0 - jnp.exp(count * math.log(0.9)))[:, 0:1]
    fix_two = (1.0 - jnp.exp(count * math.log(0.999)))[:, 0:1]

    def update(index, grad):
        entry = [ref[...] for ref in state[3 * index : 3 * index + 3]]
        values = adam_update(*entry, grad, clip_factor, fix_one, fix_two, step_rates[index],
                             decay_rates[index])
        for ref, value in zip(new[3 * index : 3 * index + 3], values):
            ref[...] = value

    update(0, ada_ref[...])
    update(4, up_ref[...])
    update(5, down_ref[...])

    @pl.when(i < 3)
    def _():
        update(2, qkv_ref[...][None])

    @pl.when(i == 3)
    def _():
        update(1, norm_ref[:, : state[3].shape[1]])
        update(3, out_ref[...])


def update_stage(half, step, input_rows, result, result_far, sums, state, token_total):
    rows, width = result.shape
    middle_sum, qkv_sum, out_sum, ada_sum, norm_sum, squares = sums
    ada_sum = ada_sum.reshape(-1, ada_sum.shape[-1])
    steps = 4
    blocks = steps // 2
    size = rows // blocks
    hidden = middle_sum.shape[1] // 2

    def side(match, lead):
        def index(i, half, step):
            same = (i // blocks == half[0]) == match
            at = jnp.where(same, i % blocks, jnp.where(i < blocks, 0, blocks - 1))
            return lead + (at, 0)

        return index

    block = (size, width)
    out = pl.BlockSpec(block, lambda i, half, step: (i, 0))
    fixed = lambda entry: pl.BlockSpec(entry.shape, lambda *_, n=entry.ndim: (0,) * n)
    slab = pl.BlockSpec((state[12].shape[0], hidden // steps), lambda i, *_: (0, i))
    next_slab = pl.BlockSpec((state[12].shape[0], hidden // steps), lambda i, *_: (0, steps + i))
    third = (state[6].shape[1], state[6].shape[2])
    qkv_spec = pl.BlockSpec((1,) + third, lambda i, *_: (jnp.minimum(i, 2), 0, 0))
    ada_spec = pl.BlockSpec((ada_sum.shape[0] // steps, ada_sum.shape[1]), lambda i, *_: (i, 0))
    specs = (
        [ada_spec] * 3 + [fixed(state[3])] * 3 + [qkv_spec] * 3 + [fixed(state[9])] * 3
        + [slab] * 6
    )
    return pl.pallas_call(
        functools.partial(update_kernel, token_total=token_total),
        grid_spec=pltpu.PrefetchScalarGridSpec(
            num_scalar_prefetch=2,
            grid=(steps,),
            in_specs=[
                pl.BlockSpec((1,) + block, side(True, (0,))),
                pl.BlockSpec((1,) + block, side(False, (1,))),
                pl.BlockSpec(block, side(True, ())),
                pl.BlockSpec(block, side(False, ())),
                slab, next_slab,
                pl.BlockSpec(third, lambda i, *_: (0, jnp.minimum(i, 2))),
                fixed(out_sum), ada_spec, fixed(norm_sum), fixed(squares),
            ] + specs,
            out_specs=[out, out, pl.BlockSpec((1, LANES), lambda *_: (0, 0))] + specs,
        ),
        out_shape=[shape_of((2 * rows, width), F32), shape_of((2 * rows, width), BF),
                   shape_of((1, LANES), F32)]
        + [shape_of(entry.shape, F32) for entry in state],
        compiler_params=params(),
        name="update_stage",
    )(half, step, input_rows, input_rows, result, result_far, middle_sum, middle_sum, qkv_sum,
      out_sum, ada_sum, norm_sum, squares, *state)


def factors(count):
    return (count // 4, 2, 2)


def swap_mp(value):
    return lax.ppermute(value, "mp", [(0, 1), (1, 0)])


def swap_dp(value, distance):
    count = lax.axis_size("dp")
    return lax.ppermute(value, "dp", [(i, i ^ distance) for i in range(count)])


def turn_dp(value, distance):
    count = lax.axis_size("dp")
    return lax.ppermute(value, "dp", [(i, (i + distance) % count) for i in range(count)])


def pick(value, index, axis):
    return lax.dynamic_index_in_dim(value, index, axis, keepdims=False)


def scatter_sum(parts, order):
    count = lax.axis_size("dp")
    outer, mid, inner = factors(count)
    me = lax.axis_index("dp")
    place = {4: me // 4, 2: (me // 2) % 2, 1: me % 2}

    def widen(part):
        return part.reshape((outer, mid, inner) + part.shape[1:]).astype(F32)

    total = widen(parts[0])
    for part in parts[1:]:
        total = total + widen(part)
    for distance in order:
        axis = 1 if (distance == 2 or total.ndim == 4) else 2
        gone = pick(total, 1 - place[distance], axis).astype(BF)
        total = pick(total, place[distance], axis) + swap_dp(gone, distance).astype(F32)
    arrived = [
        turn_dp(pick(total, (place[4] + hop) % outer, 0).astype(BF), 4 * hop)
        for hop in range(1, outer)
    ]
    total = pick(total, place[4], 0)
    for piece in arrived:
        total = total + piece.astype(F32)
    return total


def scatter_halves(near, far_sum):
    count = lax.axis_size("dp")
    width, columns = near.shape
    cut = columns // 2 // LANES * LANES
    shards = lambda value: value.reshape(count, width // count, value.shape[1])
    first = scatter_sum([shards(near[:, :cut]), shards(far_sum[:, :cut])], (2, 1))
    second = scatter_sum([shards(near[:, cut:]), shards(far_sum[:, cut:])], (1, 2))
    return jnp.concatenate([first, second], axis=1)


def sum_everywhere(value):
    value = value + swap_mp(value)
    distance = 1
    while distance < lax.axis_size("dp"):
        value = value + swap_dp(value, distance)
        distance *= 2
    return value


def in_order(half, near, far):
    first = jnp.where(half == 0, near, far)
    second = jnp.where(half == 0, far, near)
    return jnp.concatenate([first, second], axis=0)


def per_device(
    tokens, cond, segments, out_grad, step,
    ada_weight, ada_first, ada_second,
    norm_params, norm_first, norm_second,
    qkv_weight, qkv_first, qkv_second,
    out_weight, out_first, out_second,
    up_weight, up_first, up_second,
    down_weight, down_first, down_second,
):
    count = lax.axis_size("dp")
    width = tokens.shape[1]
    rows = tokens.shape[0] // 2
    conds = cond.shape[1]
    part = width // count
    half = lax.axis_index("mp")
    half_ref = half.reshape(1).astype(jnp.int32)
    token_total = float(tokens.shape[0] * count)

    fused = count == 16 and part % 16 == 0 and ada_weight.shape[1] % 32 == 0
    if fused:
        (h_one, queries, keys, values, mixed, near, far, wa, cosines, sines, query_lanes,
         key_lanes, up_near, up_far, down_near, down_far, lse, norms) = opening(
            count, tokens, cond, segments, rope_constants(rows),
            (ada_weight.T, norm_params, qkv_weight, out_weight.T, up_weight, down_weight.T),
        )
        wa = wa.reshape(-1, conds)
        features, tables = (query_lanes, key_lanes), (cosines, sines)
    else:
        ada_shard = ada_weight.T.astype(BF)
        small_shard = jnp.concatenate(
            [
                qkv_weight.astype(BF).transpose(1, 0, 2).reshape(part, -1),
                jnp.pad(norm_params.astype(BF).T, ((0, 0), (0, LANES - 8))),
            ],
            axis=1,
        )
        down_shard = jnp.concatenate([down_weight.astype(BF).T, out_weight.astype(BF).T], axis=1)
        segment = pick(segments, half, 0)
        features = document_features(segment)
        tables = rope_tables(rows)
        wa = lax.all_gather(ada_shard, "dp", axis=0, tiled=True)
        near = lax.all_gather(small_shard, "dp", axis=0, tiled=True)
        far = swap_mp(near)
        norms = near[:, -LANES:].T[:8].astype(F32)
        up_near = lax.all_gather(up_weight.astype(BF), "dp", axis=0, tiled=True)
        down_near = lax.all_gather(down_shard, "dp", axis=0, tiled=True)
        up_far, down_far = swap_mp(up_near), swap_mp(down_near)
        h_one, queries, keys, values = first_stage(
            half_ref, tokens, cond, wa, norms, near, far, tables
        )
        mixed, lse = attend(queries, keys, values, segment, features)
    result, dx, upstream, z, gy, h_two, du, ga, dwa_two, dp_two = middle_stage(
        half_ref, tokens, out_grad, cond, mixed, wa, norms, up_near, up_far, down_near, down_far
    )
    result_far = swap_mp(result)

    block = width // 2
    if fused:
        *grads, last, middle_sum = spread(
            count, h_two, gy, ga, du, z, mixed, queries, keys, values, upstream, lse, features,
            tables,
        )
    else:
        steps = du.shape[1] // 2 // block

        def middle_grads(which, name):
            return weight_grads(
                [gy, h_two, ga], [du, z, mixed],
                [(steps, 1, 0, which * steps), (steps, 0, 1, which * steps), (1, 2, 2, which)],
                block, name,
            )

        middle_far = swap_mp(middle_grads(1, "middle_grads_far"))
        middle_near = middle_grads(0, "middle_grads_near")
        middle_sum = scatter_halves(middle_near, middle_far)
        grads = attend_back(
            queries, keys, values, upstream, mixed, lse, segment, features, tables
        )

    if fused:
        input_rows, first_sum, out_sum, ada_halves, norm_sum, squares = closing(
            count, tokens, cond, h_one, grads, dx, wa, norms, near, far, dwa_two, dp_two,
            last, middle_sum, token_total,
        )
        turn = lambda group: tuple(entry.T for entry in group)
        ada_state = (ada_weight, ada_first, ada_second)
        out_state = (out_weight, out_first, out_second)
        down_state = (down_weight, down_first, down_second)
        state = (
            *turn(ada_state), norm_params, norm_first, norm_second,
            qkv_weight, qkv_first, qkv_second, *turn(out_state), up_weight, up_first, up_second,
            *turn(down_state),
        )
        input_grad, result, grad_norm, *new = update_stage(
            half_ref, step, input_rows, result, result_far,
            (middle_sum, first_sum, out_sum, ada_halves, norm_sum, squares), state, token_total,
        )
        return (
            result, input_grad, grad_norm[0, :1],
            *turn(new[:3]), *new[3:9], *turn(new[9:12]), *new[12:15], *turn(new[15:]),
        )

    def first_grads(which, name):
        return weight_grads(
            [h_one], list(grads), [(1, 0, index, which) for index in range(3)], block, name
        )

    first_far = swap_mp(first_grads(1, "first_grads_far"))
    first_near = first_grads(0, "first_grads_near")
    first_sum = scatter_halves(first_near, first_far)

    input_grad, dwa_one, dp_one = last_stage(
        half_ref, tokens, cond, dx, grads, wa, norms, near, far
    )
    input_far = swap_mp(input_grad)

    dwa = jnp.concatenate([dwa_one, dwa_two], axis=1)
    ada_cols = dwa.shape[1] // count
    dwa_rows = dwa[:conds].T.astype(BF).reshape(count, 2, ada_cols // 2, conds)
    norm_rows = jnp.concatenate(
        [dp_one[0:1], dp_two[0:1], dwa[conds].reshape(6, width)], axis=0
    ).astype(BF)
    norm_rows = norm_rows.reshape(8, count, part).transpose(1, 0, 2)
    norm_rows = jnp.pad(norm_rows, ((0, 0), (0, 0), (0, conds - part)))
    ada_near = jnp.concatenate([pick(dwa_rows, half, 1), norm_rows], axis=1)
    ada_far = swap_mp(jnp.concatenate([pick(dwa_rows, 1 - half, 1), norm_rows], axis=1))
    ada_sum = scatter_sum([ada_near, ada_far], (2, 1))
    ada_half, norm_sum = ada_sum[: ada_cols // 2], ada_sum[ada_cols // 2 :, :part]
    ada_rows = in_order(half, ada_half, swap_mp(ada_half))

    wide_cols = du.shape[1] // 2
    up_mean = middle_sum[:, :wide_cols] / token_total
    down_mean = middle_sum[:, wide_cols : 2 * wide_cols] / token_total
    out_mean = middle_sum[:, 2 * wide_cols :] / token_total
    qkv_mean = first_sum / token_total
    ada_mean = ada_rows / token_total
    norm_mean = norm_sum / token_total
    local_sq = (
        jnp.sum(qkv_mean * qkv_mean)
        + jnp.sum(out_mean * out_mean)
        + jnp.sum(up_mean * up_mean)
        + jnp.sum(down_mean * down_mean)
        + 0.5 * (jnp.sum(ada_mean * ada_mean) + jnp.sum(norm_mean * norm_mean))
    )
    grad_norm = jnp.sqrt(sum_everywhere(jnp.full((8, LANES), local_sq, F32))[0, 0])
    clip_factor = jnp.minimum(1.0, clip_limit / (grad_norm + 1e-06))
    step_count = step[0].astype(F32)
    fix_one = 1.0 - jnp.exp(step_count * math.log(0.9))
    fix_two = 1.0 - jnp.exp(step_count * math.log(0.999))

    ada_grad = ada_mean.T
    qkv_grad = qkv_mean.reshape(part, 3, -1).transpose(1, 0, 2)
    state = (
        (ada_weight, ada_first, ada_second, ada_grad),
        (norm_params, norm_first, norm_second, norm_mean),
        (qkv_weight, qkv_first, qkv_second, qkv_grad),
        (out_weight, out_first, out_second, out_mean.T),
        (up_weight, up_first, up_second, up_mean),
        (down_weight, down_first, down_second, down_mean.T),
    )
    outputs = [
        in_order(half, result, result_far),
        in_order(half, input_grad, input_far),
        grad_norm.reshape(1),
    ]
    for index, entry in enumerate(state):
        outputs += adam_update(
            *entry, clip_factor, fix_one, fix_two, step_rates[index], decay_rates[index]
        )
    return tuple(outputs)


def solution(mesh):
    column = (P(None, "dp"),) * 3
    weights = (
        column
        + column
        + (P(None, "dp", "mp"),) * 3
        + (P("mp", "dp"),) * 3
        + (P("dp", "mp"),) * 3
        + (P("mp", "dp"),) * 3
    )
    row = P("dp", None)
    return jax.shard_map(
        per_device,
        mesh=mesh,
        in_specs=(row, row, row, row, P()) + weights,
        out_specs=(row, row, P()) + weights,
        check_vma=False,
    )
```

profile of v0, /device:TPU:0, one launch (start us, length us, event | category | flops | bytes accessed | tf_op | source)
XLA Modules:
  0.0 258.7 jit_solution(2430868910184395586)
XLA Ops:
  0.7 84.7 %opening.1 = (bf16[1024,768]{1,0:T(8,128)(2,1)}, bf16[1024,768]{1,0:T(8,128)(2,1)}, bf16[1024,768]{1,0:T(8,128)(2,1)}, bf16[1024,768]{1,0:T(8,128)(2,1)}, bf16[1...) custom-call(bf16[2048,768]{1,0:T(8,128)(2,1)} %tok_ref.3, ...), custom_call_target="tpu_custom_call" | custom-call | tf_op jit(solution)/shard_map/opening/pallas_call | solution.py:924
  85.4 42.3 %middle_stage.1 = (bf16[1024,768]{1,0:T(8,128)(2,1)}, f32[1024,768]{1,0:T(8,128)}, bf16[1024,768]{1,0:T(8,128)(2,1)}, bf16[1024,3072]{1,0:T(8,128)(2,1)}, bf16[1...) custom-call(s32[1]{0:T(128)} %bitcast.half, ...), custom_call_target="tpu_custom_call" | custom-call | tf_op jit(solution)/shard_map/middle_stage/pallas_call | solution.py:421
  127.6 0.6 collective-permute-start
  128.9 67.0 %spread.1 = (bf16[1024,768]{1,0:T(8,128)(2,1)}, bf16[1024,768]{1,0:T(8,128)(2,1)}, bf16[1024,768]{1,0:T(8,128)(2,1)}, bf16[4,2,2,48,384]{4,3,2,1,0:T(8,128)(2,1)}, f32[48,3072]{1,0:T(8,128)}) custom-call(bf16[1024,768]{1,0:T(8,128)(2,1)} %get-tuple-element.89.h_in, bf16[1024,768]{1,0:T(8,128)(2,1)} %get-tuple-element.90.gy_in, ...), custom_call_target="tpu_custom_call" | custom-call | tf_op jit(solution)/shard_map/spread/pallas_call | solution.py:1287
  195.9 50.6 %closing.1 = (f32[2,1024,768]{2,1,0:T(8,128)}, f32[48,1152]{1,0:T(8,128)}, f32[48,384]{1,0:T(8,128)}, f32[2,144,128]{2,1,0:T(8,128)}, f32[8,128]{1,0:T(8,128)}, /*index=5*/f32[8,128]{1,0:T(8,128)}) custom-call(bf16[2048,768]{1,0:T(8,128)(2,1)} %tok_ref.3, bf16[2048,128]{1,0:T(8,128)(2,1)} %cond_ref.3, bf16[1024,768]{1,0:T(8,128)(2,1)} %get-tuple-element.81.h_in, ...), custom_call_target="tpu_custom_call" | custom-call | tf_op jit(solution)/shard_map/closing/pallas_call | solution.py:1579
  246.4 0.0 collective-permute-done.resb_ref
  246.5 0.0 copy-start
  246.5 1.1 copy-done
  247.6 10.9 %update_stage.1 = (f32[2048,768]{1,0:T(8,128)}, bf16[2048,768]{1,0:T(8,128)(2,1)}, f32[1,128]{1,0:T(1,128)}, f32[288,128]{1,0:T(8,128)}, f32[288,128]{1,0:T(8,12...) custom-call(s32[1]{0:T(128)} %bitcast.half, ...), custom_call_target="tpu_custom_call" | custom-call | tf_op jit(solution)/shard_map/update_stage/pallas_call | solution.py:1691
Async XLA Ops:
  127.6 118.8 %collective-permute-start = (bf16[1024,768]{1,0:T(8,128)(2,1)}, bf16[1024,768]{1,0:T(8,128)(2,1)S(1)}, u32[]{:S(2)}, u32[]{:S(2)}) collective-permute-start(bf16[1024,768]{1,0:T(8,128)(2,1)} %get-tuple-element.114.resa_ref), channel_id=1, source_target_pairs={{0,1},{1,0},{2,3},{3,2},{4,5},{5,4},{6,7},{7,6},{8,9},{9,8},{10,11... | collective-permute-start | bytes 4718600 | tf_op jit(solution)/shard_map/ppermute | solution.py:1721
  246.5 1.1 copy-start
where the time goes:
time: 259 us
  Pallas kernels  255 us (98%)
    pallas_call x1, Pallas kernels, opening(): pl.pallas_call(functools.partial(opening_kernel, count=count, cuts=cuts,...  84.7 us
    pallas_call x1, Pallas kernels, spread(): pl.pallas_call(functools.partial(spread_kernel, count=count, bk=256), in_...  67 us
    pallas_call x1, Pallas kernels, closing(): pl.pallas_call(functools.partial(closing_kernel, count=count, token_total...  50.6 us
    pallas_call x1, Pallas kernels, middle_stage(): pl.pallas_call(functools.partial(middle_kernel, chunk=768), grid_spec=plt...  42.3 us
    pallas_call x1, Pallas kernels, update_stage(): pl.pallas_call(functools.partial(update_kernel, token_total=token_total),...  10.9 us
  transfers between devices with their start and end apart: 1, of which 0 were waited for; matrix products, arithmetic and copies ran while one was open for 0% of the time, Pallas kernels for 45%

commit v1 on v0

--- a/solution.py
+++ b/solution.py
@@ -350,31 +350,33 @@
     gain = p_ref[1:2, :]
     spread = 1.0 + scale
     h = (normal * gain * spread + shift).astype(BF)
-    h_ref[...] = h
+    h_ref[...] = h.T
 
     @pl.when(pl.program_id(0) == 0)
     def _():
         for load in loads:
             load.wait()
 
+    root = math.sqrt(2.0 / math.pi)
     out = jnp.zeros_like(middle)
     for start, up_ref, down_ref in ((0, w1a_ref, w2a_ref), (hidden, w1b_ref, w2b_ref)):
         for at in range(0, hidden, chunk):
             u = dot(h, up_ref[:, at : at + chunk])
             square = u * u
-            flat = jnp.tanh(math.sqrt(2.0 / math.pi) * u * (1.0 + 0.044715 * square))
-            half_up = 0.5 * (1.0 + flat)
+            flat = jnp.tanh(u * (0.044715 * root * square + root))
+            half_up = 0.5 * flat + 0.5
             z = (u * half_up).astype(BF)
             z_ref[:, start + at : start + at + chunk] = z
-            slope[:, start + at : start + at + chunk] = half_up + 0.5 * u * (
-                1.0 - flat * flat
-            ) * (math.sqrt(2.0 / math.pi) * (1.0 + 3.0 * 0.044715 * square))
+            bend = u * (6.0 * 0.044715 * root * square + 2.0 * root)
+            slope[:, start + at : start + at + chunk] = (
+                half_up * (bend * (1.0 - half_up) + 1.0)
+            ).astype(slope.dtype)
             out = out + dot(z, down_ref[:, at : at + chunk], NT)
 
     g = g_ref[...].astype(F32)
     res_ref[...] = (middle + gate_two * out).astype(BF)
     gy = (gate_two * g).astype(BF)
-    gy_ref[...] = gy
+    gy_ref[...] = gy.T
     dgate_two = (g * out).astype(BF)
 
     dh = jnp.zeros_like(middle)
@@ -389,7 +391,7 @@
     dx = g + norm_backward(dh * gain * spread, normal, rstd)
     dx_ref[...] = dx
     ga = (gate_one * dx).astype(BF)
-    ga_ref[...] = ga
+    ga_ref[...] = ga.T
     do_ref[:, :own] = dot(ga, woa_ref[...]).astype(BF)
     do_ref[:, own:] = dot(ga, wob_ref[...]).astype(BF)
 
@@ -416,6 +418,8 @@
     row = pl.BlockSpec((ROW_BLOCK, width), plain)
     wide = pl.BlockSpec((ROW_BLOCK, 2 * hidden), plain)
     narrow = shape_of((rows, width), BF)
+    turned = pl.BlockSpec((width, ROW_BLOCK), lambda i, half: (0, i))
+    tall = shape_of((width, rows), BF)
     broad = shape_of((rows, 2 * hidden), BF)
     total = (cond.shape[1] + 16, 4 * width)
     return pl.pallas_call(
@@ -434,15 +438,15 @@
                 resident((width, width // 2), (0, 2 * hidden // width)),
                 *[pl.BlockSpec(memory_space=pl.ANY)] * 4,
             ],
-            out_specs=[row, row, row, wide, row, row, wide, row,
+            out_specs=[row, row, row, wide, turned, turned, wide, turned,
                        pl.BlockSpec(total, lambda i, half: (0, 0)),
                        pl.BlockSpec((8, width), lambda i, half: (0, 0))],
             scratch_shapes=[pltpu.VMEM((ROW_BLOCK, 2 * hidden), F32)]
             + [pltpu.VMEM((width, hidden), BF)] * 4
             + [pltpu.SemaphoreType.DMA((4,))],
         ),
-        out_shape=[narrow, shape_of((rows, width), F32), narrow, broad, narrow, narrow, broad,
-                   narrow, shape_of(total, F32), shape_of((8, width), F32)],
+        out_shape=[narrow, shape_of((rows, width), F32), narrow, broad, tall, tall, broad,
+                   tall, shape_of(total, F32), shape_of((8, width), F32)],
         compiler_params=params(),
         name="middle_stage",
     )(half, tokens, out_grad, cond, mixed, wa, norms, down_near, down_far, up_near, up_far,
@@ -755,10 +759,14 @@
     downs.phase_one(0)
     each("phase_one", 1)
     fine = cosb_ref.shape[0]
-    for step in range(cosa_ref.shape[0]):
-        at, row = slice(step * fine, (step + 1) * fine), slice(step, step + 1)
+
+    def rope_rows(step, _):
+        at, row = pl.ds(pl.multiple_of(step * fine, fine), fine), pl.ds(step, 1)
         cos_ref[at, :] = cosa_ref[row, :] * cosb_ref[...] - sina_ref[row, :] * sinb_ref[...]
         sin_ref[at, :] = sina_ref[row, :] * cosb_ref[...] + cosa_ref[row, :] * sinb_ref[...]
+        return 0
+
+    lax.fori_loop(0, cosa_ref.shape[0], rope_rows, 0)
     each("phase_one", 2)
     each("phase_two", 1)
     documents = seg_ref[pl.ds(core, 1), :].astype(F32)
@@ -798,22 +806,27 @@
         if tick == 0:
             ups.phase_two(1)
             ups.phase_one(2)
-        if tick == 2:
+        if tick == 1:
             ups.phase_one(3)
             ups.phase_two(2)
+        if tick == 3:
+            ups.phase_two(3)
         if tick == 4:
-            ups.phase_two(3)
             downs.phase_two(1)
             ups.phase_swap(0)
+        if tick == 5:
+            ups.phase_swap(1)
+            downs.phase_swap(0)
         if tick == 6:
             downs.phase_two(2)
-            downs.phase_swap(0)
-            ups.phase_swap(1)
+            ups.phase_swap(2)
         if tick == 7:
-            ups.phase_swap(2)
+            ups.phase_swap(3)
+        if tick == 8:
+            downs.phase_two(3)
             downs.phase_swap(1)
-        if tick == 8:
-            ups.phase_swap(3)
+        if tick == 9:
+            downs.phase_swap(2)
 
     def row_block(i, _):
         at = pl.ds(pl.multiple_of(i * ROW_BLOCK, ROW_BLOCK), ROW_BLOCK)
@@ -822,7 +835,7 @@
         scale = dot(cond, wa[width : 2 * width], NT) + table_ref[3:4, :]
         normal, _ = normalize(x_vm[at, :].astype(F32))
         h = (normal * table_ref[0:1, :] * (1.0 + scale) + shift).astype(BF)
-        h_ref[at, :] = h
+        h_ref[:, at] = h.T
         cos = jnp.concatenate([cos_ref[at, :]] * (own // LANES), axis=1)
         sin = jnp.concatenate([sin_ref[at, :]] * (own // LANES), axis=1)
         for first, w_ref in ((0, near_ref), (own, far_ref)):
@@ -890,8 +903,6 @@
         return 0
 
     lax.fori_loop(0, width // LANES, head_pair, 0)
-    downs.phase_two(3)
-    downs.phase_swap(2)
     downs.phase_swap(3)
     keep(width // LANES - 1).wait()
     for save in saves.values():
@@ -918,7 +929,7 @@
     pairs = width // LANES
     pair = pltpu.VMEM((2, rows, LANES), BF)
     half_cols = ada.shape[0] // 2
-    kept = [act] * 5 + [small, small, shape_of((count, 2, half_cols, conds), BF), table, table,
+    kept = [shape_of((width, rows), BF)] + [act] * 4 + [small, small, shape_of((count, 2, half_cols, conds), BF), table, table,
                         feature, feature]
     cuts = (512, hidden // 2, second.shape[1] // 2 // LANES * LANES)
     return pl.pallas_call(
@@ -1043,7 +1054,7 @@
                   dq_out, dk_out, dv_out, last_ref, sum_ref,
                   h_ref, gy_ref, ga_ref, o_ref, q_ref, k_ref, v_ref, do_ref, lse_ref,
                   fq_ref, fk_ref, cos_ref, sin_ref, dq_ref, dk_ref, dv_ref,
-                  h_turn, gy_turn, ga_turn, right, far6, sum6, one6, two6, hop6, far1,
+                  right, far6, sum6, one6, two6, hop6, far1,
                   qz, kz, qm, dm, vm, kt, delta, dqt,
                   load_sems, input_sems, keep_sems, sems, *, count, bk):
     place = my_place(count)
@@ -1093,12 +1104,11 @@
             sum_ref[:, at : at + columns] = entry.finish()
             at += columns
 
-    lefts, sources = (h_turn, gy_turn), (du_ref, z_ref)
-    groups = [(side, index) for index in range(2) for side in (1, 0)]
-
-    def load(group, b):
-        side, index = groups[group]
-        at = pl.multiple_of(side * (span // 2) + b * block, block)
+    lefts, sources = (h_ref, gy_ref), (du_ref, z_ref)
+
+    def load(index, turn):
+        b = lax.rem(turn, each)
+        at = pl.multiple_of((1 - turn // each) * (span // 2) + b * block, block)
         return pltpu.make_async_copy(
             sources[index].at[:, pl.ds(at, block)], right.at[b], load_sems.at[b]
         )
@@ -1112,58 +1122,53 @@
     for item in inputs[4:]:
         item.start()
     inputs[0].wait()
-    h_turn[...] = h_ref[...].T
     meet(others)
 
-    for group, (side, index) in enumerate(groups):
-
-        def grad_block(b, _):
-            load(group, b).wait()
+    for index in range(2):
+
+        def grad_block(turn, _):
+            b = lax.rem(turn, each)
+            load(index, turn).wait()
             grad = dot(lefts[index][...], right[b])
-            if group + 1 < len(groups):
-                load(group + 1, b).start()
-            j = index * each + b
-            if side:
-                far6[j] = grad.reshape(shards).astype(BF)
-            for b_static in range(each):
-                at = index * each + b_static
-
-                @pl.when(b == b_static)
+
+            @pl.when(turn < each)
+            def _():
+                load(index, turn + each).start()
+                far6[index * each + b] = grad.reshape(shards).astype(BF)
+
+            for step in range(each):
+
+                @pl.when(turn == step)
                 def _():
-                    if side:
-                        swaps[at].start()
-                    else:
-                        swaps[at].wait_recv()
-
-            if not side:
-                sum6[j] = (grad.reshape(shards) + sum6[j].astype(F32)).astype(BF)
-                if index == 0:
-                    for b_static in range(2):
-
-                        @pl.when(b == b_static)
-                        def _():
-                            start(b_static)
+                    swaps[index * each + step].start()
+
+                @pl.when(turn == each + step)
+                def _():
+                    if index == 0:
+                        load(1, step).start()
+                    at = index * each + step
+                    swaps[at].wait_recv()
+                    sum6[at] = (grad.reshape(shards) + sum6[at].astype(F32)).astype(BF)
+                    if at < 2:
+                        start(at)
 
             return 0
 
-        if index == 1 and side:
+        if index:
             inputs[1].wait()
-            gy_turn[...] = gy_ref[...].T
-        lax.fori_loop(0, each, grad_block, 0)
-        if index == 1 and side:
-            inputs[2].wait()
-            inputs[3].wait()
-            ga_turn[...] = ga_ref[...].T
-            grad = dot(ga_turn[...], o_ref[:, own:])
-            far1[...] = grad.reshape(tail).astype(BF)
-            swaps[-1].start()
-            phase_two(0)
+        lax.fori_loop(0, 2 * each, grad_block, 0)
+        if index == 0:
             start(2)
-    grad = dot(ga_turn[...], o_ref[:, :own])
+    inputs[2].wait()
+    inputs[3].wait()
+    phase_two(0)
+    start(3)
+    far1[...] = dot(ga_ref[...], o_ref[:, own:]).reshape(tail).astype(BF)
+    swaps[-1].start()
+    phase_two(1)
+    grad = dot(ga_ref[...], o_ref[:, :own])
     swaps[-1].wait_recv()
     last_ref[...] = (grad.reshape(tail) + last_ref[...].astype(F32)).astype(BF)
-    phase_two(1)
-    start(3)
     for item in inputs[4:]:
         item.wait()
 
@@ -1172,7 +1177,7 @@
             phase_two(p + 2)
         if p < 2:
             start(p + 4)
-        if p < 5:
+        if p < 4:
             phase_hops(p)
         if p == 4:
             phase_hops(5)
@@ -1209,8 +1214,8 @@
         delta[1:2, :] = jnp.sum(product[HEAD_DIM:], axis=0, keepdims=True)
         dqt[...] = jnp.zeros_like(dqt)
 
-        def key_block(j, reach):
-            at = pl.ds(pl.multiple_of(j * bk, bk), bk)
+        def key_block(first, reach):
+            at = slice(first, first + bk)
             dk = jnp.zeros((bk, LANES), F32)
             dv = jnp.zeros((bk, LANES), F32)
             scores = [dot(kz[h, at, :], qz[h, reach, :], NT) for h in range(2)]
@@ -1225,21 +1230,15 @@
             dk_ref[at, lanes] = unrotate(dk, at)
             dv_ref[at, lanes] = dv.astype(BF)
 
-        reaches = {}
         for first in range(0, rows, bk):
             low = max(0, (first - rows // 2 + 1) // LANES * LANES)
             high = min(rows, -(-(first + bk + rows // 2 - 1) // LANES) * LANES)
-            reaches.setdefault((low, high), []).append(first // bk)
-        for (low, high), blocks in reaches.items():
-
-            def one_block(j, _):
-                key_block(j, slice(low, high))
-                return 0
-
-            if len(blocks) == 1:
-                key_block(blocks[0], slice(low, high))
-            else:
-                lax.fori_loop(blocks[0], blocks[-1] + 1, one_block, 0)
+            key_block(first, slice(low, high))
+            if first + bk == rows // 2:
+
+                @pl.when(p == 4)
+                def _():
+                    phase_hops(4)
 
         dq_ref[:, lanes] = unrotate(dqt[...].T * HEAD_DIM**-0.5, pl.ds(0, rows))
 
@@ -1280,7 +1279,6 @@
     hbm = pl.BlockSpec(memory_space=pl.ANY)
     act = shape_of((rows, width), BF)
     last = shape_of((outer, 2, 2, part, width // 2), BF)
-    turn = pltpu.VMEM((width, rows), BF)
     pair = pltpu.VMEM((2, rows, LANES), BF)
     copies = 7 + 12 * (2 + outer - 1)
     held = [h_two, gy, ga, mixed, queries, keys, values, upstream, lse, *features, *tables]
@@ -1290,7 +1288,7 @@
         out_specs=[hbm] * 3 + [vm] * 2,
         out_shape=[act, act, act, last, shape_of((part, 2 * hidden), F32)],
         scratch_shapes=[pltpu.VMEM(entry.shape, entry.dtype) for entry in held + [act] * 3]
-        + [turn, turn, turn, pltpu.VMEM((each, rows, block), BF)]
+        + [pltpu.VMEM((each, rows, block), BF)]
         + scatter_buffers(outer, 2 * each, part, block)
         + [pltpu.VMEM(last.shape, BF)]
         + [pair] * 5
@@ -1314,7 +1312,7 @@
                    dwa_two_in, dx_in, last_in, mid_ref, p_ref, dp_two_ref,
                    rows_ref, qkv_ref, out_ref, ada_ref, norm_ref, square_ref,
                    h_ref, grads, x_vm, c_vm, near_ref, far_ref, wa_ref, dwa_two_ref, dx_ref,
-                   turned, mine, dh_vm, dwa_vm, dp_vm, dwt, plane, column,
+                   mine, dh_vm, dwa_vm, dp_vm, dwt, plane, column,
                    far3, sum3, one3, two3, hop3, sum2, one2, two2, hop2,
                    sum1, one1, two1, hop1, local, sems, *, count, token_total):
     place = my_place(count)
@@ -1340,8 +1338,9 @@
         pltpu.make_async_copy(src, dst, local.at[index])
         for index, (src, dst) in enumerate(pieces)
     ]
+    loads[9].start()
     loads[11].start()
-    for load in loads[:11]:
+    for load in loads[:9] + loads[10:11]:
         load.start()
 
     swaps = [across_cores(place, far3.at[c], sum3.at[c], sems) for c in range(3)]
@@ -1393,27 +1392,18 @@
         for entry in scatters[c]:
             getattr(entry, method)()
 
-    loads[0].wait()
-    turned[...] = h_ref[...].T
-    meet(others)
-    loads[11].wait()
-    all_of(3, "start")
+    def project(c):
+        if c < 2:
+            loads[1 + c].wait()
+        grad = dot(h_ref[...], grads[c])
+        far3[c] = grad[:, own:].reshape(shards).astype(BF)
+        swaps[c].start()
+        mine[c] = grad[:, :own].reshape(shards)
 
     def add_near_grad(c):
         swaps[c].wait_recv()
         sum3[c] = (mine[c] + sum3[c].astype(F32)).astype(BF)
         all_of(c, "start")
-
-    for c in range(3):
-        loads[1 + c].wait()
-        grad = dot(turned[...], grads[c])
-        far3[c] = grad[:, own:].reshape(shards).astype(BF)
-        swaps[c].start()
-        mine[c] = grad[:, :own].reshape(shards)
-        if c:
-            add_near_grad(c - 1)
-    for load in loads[4:10]:
-        load.wait()
 
     def place_rows(start, values):
         at = 0
@@ -1426,6 +1416,7 @@
             ]
             at += high - low
 
+    loads[9].wait()
     place_rows(2 * width, dwa_two_ref[:conds, :].T.astype(BF))
     dwa_vm[...] = jnp.zeros_like(dwa_vm)
     dp_vm[...] = jnp.zeros_like(dp_vm)
@@ -1434,6 +1425,17 @@
         dp_vm[4 + block : 5 + block, :] = dwa_two_ref[
             conds : conds + 1, block * width : (block + 1) * width
         ]
+    loads[0].wait()
+    meet(others)
+    loads[11].wait()
+    all_of(3, "start")
+    project(0)
+    project(1)
+    add_near_grad(0)
+    loads[3].wait()
+    for load in loads[4:9]:
+        load.wait()
+
     gain = p_ref[0:1, :]
 
     def spread_of(at):
@@ -1457,17 +1459,13 @@
 
         @pl.when(i == 0)
         def _():
-            add_near_grad(2)
+            add_near_grad(1)
             all_of(3, "phase_two")
 
         @pl.when(i == 2)
         def _():
             all_of(0, "phase_two")
             all_of(3, "phase_hops")
-
-        @pl.when(i == 3)
-        def _():
-            all_of(1, "phase_two")
 
         return 0
 
@@ -1485,24 +1483,24 @@
         for side in range(2):
             dwt[shard // 4, (shard // 2) % 2, shard % 2, side, half_cols:, :] = gone
     ada_swap.start()
-    all_of(0, "phase_hops")
-    all_of(2, "phase_two")
+    all_of(1, "phase_two")
+    project(2)
     ada_swap.wait_recv()
     sum2[...] = sum2[...] + dwt[:, :, :, core]
     for entry in adas:
         entry.start()
-    all_of(1, "phase_hops")
+    add_near_grad(2)
+    all_of(0, "phase_hops")
     loads[10].wait()
 
     def events(i):
         if i == 1:
-            all_of(2, "phase_hops")
+            all_of(1, "phase_hops")
         if i == 2:
             for entry in adas:
                 entry.phase_two()
         if i == 3:
-            for entry in adas:
-                entry.phase_hops()
+            all_of(2, "phase_two")
 
     def keep(i):
         at = pl.ds(pl.multiple_of(i * ROW_BLOCK, ROW_BLOCK), ROW_BLOCK)
@@ -1526,7 +1524,10 @@
 
     lax.fori_loop(0, rows // ROW_BLOCK, second_pass, 0)
 
+    for entry in adas:
+        entry.phase_hops()
     squares = jnp.sum((mid_ref[...] / token_total) ** 2)
+    all_of(2, "phase_hops")
     for c in range(4):
         target, at = (qkv_ref, c * own) if c < 3 else (out_ref, 0)
         for entry in scatters[c]:
@@ -1589,13 +1590,12 @@
             shape_of((8, LANES), F32),
         ],
         scratch_shapes=[
-            act, pltpu.VMEM((3, rows, width), BF), act,
+            pltpu.VMEM((width, rows), BF), pltpu.VMEM((3, rows, width), BF), act,
             pltpu.VMEM((rows, conds), BF),
             half_weights, half_weights,
             pltpu.VMEM((width, conds), BF),
             pltpu.VMEM(dwa_two.shape, F32),
             pltpu.VMEM((rows, width), F32),
-            pltpu.VMEM((width, rows), BF),
             pltpu.VMEM((3, outer, 2, 2, part, width // 2), F32),
             pltpu.VMEM((rows, width), F32),
             pltpu.VMEM((conds + 16, 2 * width), F32),
@@ -1853,7 +1853,7 @@
 
         def middle_grads(which, name):
             return weight_grads(
-                [gy, h_two, ga], [du, z, mixed],
+                [gy.T, h_two.T, ga.T], [du, z, mixed],
                 [(steps, 1, 0, which * steps), (steps, 0, 1, which * steps), (1, 2, 2, which)],
                 block, name,
             )

time: 259 us -> 254 us (0.981)
  Pallas kernels: 255 us -> 251 us
    pallas_call x1, Pallas kernels: 67 us -> 63.8 us  [spread(): pl.pallas_call(functools.partial(spread_kernel, count=count, bk=256), in_...]
where the time goes in v1:
time: 254 us
  Pallas kernels  251 us (99%)
    pallas_call x1, Pallas kernels, opening(): pl.pallas_call(functools.partial(opening_kernel, count=count, cuts=cuts,...  83 us
    pallas_call x1, Pallas kernels, spread(): pl.pallas_call(functools.partial(spread_kernel, count=count, bk=256), in_...  63.8 us
    pallas_call x1, Pallas kernels, closing(): pl.pallas_call(functools.partial(closing_kernel, count=count, token_total...  51.5 us
    pallas_call x1, Pallas kernels, middle_stage(): pl.pallas_call(functools.partial(middle_kernel, chunk=768), grid_spec=plt...  41.8 us
    pallas_call x1, Pallas kernels, update_stage(): pl.pallas_call(functools.partial(update_kernel, token_total=token_total),...  10.9 us
  transfers between devices with their start and end apart: 1, of which 0 were waited for; matrix products, arithmetic and copies ran while one was open for 0% of the time, Pallas kernels for 45%

profile of v1, /device:TPU:0, one launch (start us, length us, event | category | flops | bytes accessed | tf_op | source)
XLA Modules:
  0.0 254.2 jit_solution(15599949671214317034)
XLA Ops:
  0.7 83.0 %opening.1 = (bf16[768,1024]{1,0:T(8,128)(2,1)}, bf16[1024,768]{1,0:T(8,128)(2,1)}, bf16[1024,768]{1,0:T(8,128)(2,1)}, bf16[1024,768]{1,0:T(8,128)(2,1)}, bf16[1...) custom-call(bf16[2048,768]{1,0:T(8,128)(2,1)} %tok_ref.3, ...), custom_call_target="tpu_custom_call" | custom-call | tf_op jit(solution)/shard_map/opening/pallas_call | solution.py:935
  83.7 41.8 %middle_stage.1 = (bf16[1024,768]{1,0:T(8,128)(2,1)}, f32[1024,768]{1,0:T(8,128)}, bf16[1024,768]{1,0:T(8,128)(2,1)}, bf16[1024,3072]{1,0:T(8,128)(2,1)}, bf16[7...) custom-call(s32[1]{0:T(128)} %bitcast.half, ...), custom_call_target="tpu_custom_call" | custom-call | tf_op jit(solution)/shard_map/middle_stage/pallas_call | solution.py:425
  125.5 0.6 collective-permute-start
  126.7 63.8 %spread.1 = (bf16[1024,768]{1,0:T(8,128)(2,1)}, bf16[1024,768]{1,0:T(8,128)(2,1)}, bf16[1024,768]{1,0:T(8,128)(2,1)}, bf16[4,2,2,48,384]{4,3,2,1,0:T(8,128)(2,1)}, f32[48,3072]{1,0:T(8,128)}) custom-call(bf16[768,1024]{1,0:T(8,128)(2,1)} %get-tuple-element.89.h_in, bf16[768,1024]{1,0:T(8,128)(2,1)} %get-tuple-element.90.gy_in, ...), custom_call_target="tpu_custom_call" | custom-call | tf_op jit(solution)/shard_map/spread/pallas_call | solution.py:1285
  190.5 51.5 %closing.1 = (f32[2,1024,768]{2,1,0:T(8,128)}, f32[48,1152]{1,0:T(8,128)}, f32[48,384]{1,0:T(8,128)}, f32[2,144,128]{2,1,0:T(8,128)}, f32[8,128]{1,0:T(8,128)}, /*index=5*/f32[8,128]{1,0:T(8,128)}) custom-call(bf16[2048,768]{1,0:T(8,128)(2,1)} %tok_ref.3, bf16[2048,128]{1,0:T(8,128)(2,1)} %cond_ref.3, bf16[768,1024]{1,0:T(8,128)(2,1)} %get-tuple-element.81.h_in, ...), custom_call_target="tpu_custom_call" | custom-call | tf_op jit(solution)/shard_map/closing/pallas_call | solution.py:1580
  241.9 0.0 collective-permute-done.resb_ref
  242.0 0.0 copy-start
  242.0 1.1 copy-done
  243.1 10.9 %update_stage.1 = (f32[2048,768]{1,0:T(8,128)}, bf16[2048,768]{1,0:T(8,128)(2,1)}, f32[1,128]{1,0:T(1,128)}, f32[288,128]{1,0:T(8,128)}, f32[288,128]{1,0:T(8,12...) custom-call(s32[1]{0:T(128)} %bitcast.half, ...), custom_call_target="tpu_custom_call" | custom-call | tf_op jit(solution)/shard_map/update_stage/pallas_call | solution.py:1691
Async XLA Ops:
  125.5 116.5 %collective-permute-start = (bf16[1024,768]{1,0:T(8,128)(2,1)}, bf16[1024,768]{1,0:T(8,128)(2,1)S(1)}, u32[]{:S(2)}, u32[]{:S(2)}) collective-permute-start(bf16[1024,768]{1,0:T(8,128)(2,1)} %get-tuple-element.114.resa_ref), channel_id=1, source_target_pairs={{0,1},{1,0},{2,3},{3,2},{4,5},{5,4},{6,7},{7,6},{8,9},{9,8},{10,11... | collective-permute-start | bytes 4718600 | tf_op jit(solution)/shard_map/ppermute | solution.py:1721
  242.0 1.1 copy-start

commit v2 on v1

--- a/solution.py
+++ b/solution.py
@@ -1107,11 +1107,15 @@
     lefts, sources = (h_ref, gy_ref), (du_ref, z_ref)
 
     def load(index, turn):
-        b = lax.rem(turn, each)
-        at = pl.multiple_of((1 - turn // each) * (span // 2) + b * block, block)
+        near, b = of_turn(turn)
+        at = pl.multiple_of((1 - near) * (span // 2) + b * block, block)
+        slot = lax.rem(turn, each)
         return pltpu.make_async_copy(
-            sources[index].at[:, pl.ds(at, block)], right.at[b], load_sems.at[b]
+            sources[index].at[:, pl.ds(at, block)], right.at[slot], load_sems.at[slot]
         )
+
+    def of_turn(turn):
+        return lax.rem((3 * turn + 0) // 4, 2), lax.rem((7 * turn + 0) // 4, 3)
 
     inputs[0].start()
     load(0, 0).start()
@@ -1127,26 +1131,33 @@
     for index in range(2):
 
         def grad_block(turn, _):
-            b = lax.rem(turn, each)
+            near, b = of_turn(turn)
             load(index, turn).wait()
-            grad = dot(lefts[index][...], right[b])
+            grad = dot(lefts[index][...], right[lax.rem(turn, each)])
 
             @pl.when(turn < each)
             def _():
                 load(index, turn + each).start()
+
+            if index == 0:
+
+                @pl.when(turn >= each)
+                def _():
+                    load(1, turn - each).start()
+
+            @pl.when(near == 0)
+            def _():
                 far6[index * each + b] = grad.reshape(shards).astype(BF)
 
             for step in range(each):
-
-                @pl.when(turn == step)
+                at = index * each + step
+
+                @pl.when(turn == (0, 1, 3)[step])
                 def _():
-                    swaps[index * each + step].start()
-
-                @pl.when(turn == each + step)
+                    swaps[at].start()
+
+                @pl.when(turn == (2, 4, 5)[step])
                 def _():
-                    if index == 0:
-                        load(1, step).start()
-                    at = index * each + step
                     swaps[at].wait_recv()
                     sum6[at] = (grad.reshape(shards) + sum6[at].astype(F32)).astype(BF)
                     if at < 2:
@@ -1375,18 +1386,11 @@
         at = pl.ds(i * ROW_BLOCK, ROW_BLOCK)
         row_copies.append(copy(dh_vm.at[at], rows_ref.at[1, at], (me, 1 - core)))
     ada_copy = copy(ada_ref.at[core], ada_ref.at[core], (me, 1 - core))
-    spot = 4 * core + 2 * y + x
-    plane_copies = []
-    for other in range(1, 8):
-        yy, xx = lax.rem(y + other // 2, 2), lax.rem(x + other, 2)
-        cc = lax.rem(core + other // 4, 2)
-        plane_copies.append((4 * z + 2 * yy + xx, cc))
-    beyond = [(4 * lax.rem(z + hop, outer) + 2 * y + x, core) for hop in range(1, outer)]
-
-    others = plane_copies + beyond
+    beyond = [(lax.rem(me + hop, count), core) for hop in range(1, count)]
+    others = beyond + [(me, 1 - core)]
     greet(others)
-    plane_copies = [copy(plane.at[spot], plane.at[spot], device) for device in plane_copies]
-    column_copies = [copy(column.at[z], column.at[z], device) for device in beyond]
+    plane_copies = [copy(plane.at[core], plane.at[core], (me, 1 - core))]
+    column_copies = [copy(column.at[me], column.at[me], device) for device in beyond]
 
     def all_of(c, method):
         for entry in scatters[c]:
@@ -1544,12 +1548,12 @@
     squares = squares + jnp.sum((first / token_total) ** 2)
     squares = squares + jnp.sum((second[:rest] / token_total) ** 2)
     squares = squares + 0.5 * jnp.sum((second[rest:] / token_total) ** 2)
-    plane[spot] = jnp.full((8, LANES), squares, F32)
+    plane[core] = jnp.full((8, LANES), squares, F32)
     for entry in plane_copies:
         entry.start()
     for entry in plane_copies:
         entry.wait_recv()
-    column[z] = jnp.sum(plane[...], axis=0)
+    column[me] = plane[0] + plane[1]
     for entry in column_copies:
         entry.start()
     for entry in column_copies:
@@ -1574,7 +1578,7 @@
     half_cols = wa.shape[0] // count // 2
     vm = pl.BlockSpec(memory_space=pltpu.VMEM)
     hbm = pl.BlockSpec(memory_space=pl.ANY)
-    copies = 5 + 10 * (2 + outer - 1) + rows // ROW_BLOCK + 1 + 7 + outer - 1
+    copies = 5 + 10 * (2 + outer - 1) + rows // ROW_BLOCK + 2 + count - 1
     act = pltpu.VMEM((rows, width), BF)
     half_weights = pltpu.VMEM((width, 3 * width // 2), BF)
     return pl.pallas_call(
@@ -1601,8 +1605,8 @@
             pltpu.VMEM((conds + 16, 2 * width), F32),
             pltpu.VMEM((16, width), F32),
             pltpu.VMEM((outer, 2, 2, 2, half_cols + 16, conds), BF),
-            pltpu.VMEM((8, 8, LANES), F32),
-            pltpu.VMEM((outer, 8, LANES), F32),
+            pltpu.VMEM((2, 8, LANES), F32),
+            pltpu.VMEM((count, 8, LANES), F32),
         ]
         + scatter_buffers(outer, 3, part, width // 2)
         + scatter_buffers(outer, None, half_cols + 16, conds)[1:]

time: 254 us -> 253 us (level)
  no operation moved by 1% of the time
where the time goes in v2:
time: 253 us; the launch traced here: 252 us
  Pallas kernels  249 us (98%)
    pallas_call x1, Pallas kernels, opening(): pl.pallas_call(functools.partial(opening_kernel, count=count, cuts=cuts,...  83 us
    pallas_call x1, Pallas kernels, spread(): pl.pallas_call(functools.partial(spread_kernel, count=count, bk=256), in_...  63.4 us
    pallas_call x1, Pallas kernels, closing(): pl.pallas_call(functools.partial(closing_kernel, count=count, token_total...  50.1 us
    pallas_call x1, Pallas kernels, middle_stage(): pl.pallas_call(functools.partial(middle_kernel, chunk=768), grid_spec=plt...  41.8 us
    pallas_call x1, Pallas kernels, update_stage(): pl.pallas_call(functools.partial(update_kernel, token_total=token_total),...  10.9 us
  transfers between devices with their start and end apart: 1, of which 0 were waited for; matrix products, arithmetic and copies ran while one was open for 0% of the time, Pallas kernels for 45%

profile of v2, /device:TPU:0, one launch (start us, length us, event | category | flops | bytes accessed | tf_op | source)
XLA Modules:
  0.0 252.4 jit_solution(469817654749002486)
XLA Ops:
  0.7 83.0 %opening.1 = (bf16[768,1024]{1,0:T(8,128)(2,1)}, bf16[1024,768]{1,0:T(8,128)(2,1)}, bf16[1024,768]{1,0:T(8,128)(2,1)}, bf16[1024,768]{1,0:T(8,128)(2,1)}, bf16[1...) custom-call(bf16[2048,768]{1,0:T(8,128)(2,1)} %tok_ref.3, ...), custom_call_target="tpu_custom_call" | custom-call | tf_op jit(solution)/shard_map/opening/pallas_call | solution.py:935
  83.7 41.8 %middle_stage.1 = (bf16[1024,768]{1,0:T(8,128)(2,1)}, f32[1024,768]{1,0:T(8,128)}, bf16[1024,768]{1,0:T(8,128)(2,1)}, bf16[1024,3072]{1,0:T(8,128)(2,1)}, bf16[7...) custom-call(s32[1]{0:T(128)} %bitcast.half, ...), custom_call_target="tpu_custom_call" | custom-call | tf_op jit(solution)/shard_map/middle_stage/pallas_call | solution.py:425
  125.5 0.6 collective-permute-start
  126.7 63.4 %spread.1 = (bf16[1024,768]{1,0:T(8,128)(2,1)}, bf16[1024,768]{1,0:T(8,128)(2,1)}, bf16[1024,768]{1,0:T(8,128)(2,1)}, bf16[4,2,2,48,384]{4,3,2,1,0:T(8,128)(2,1)}, f32[48,3072]{1,0:T(8,128)}) custom-call(bf16[768,1024]{1,0:T(8,128)(2,1)} %get-tuple-element.89.h_in, bf16[768,1024]{1,0:T(8,128)(2,1)} %get-tuple-element.90.gy_in, ...), custom_call_target="tpu_custom_call" | custom-call | tf_op jit(solution)/shard_map/spread/pallas_call | solution.py:1296
  190.1 50.1 %closing.1 = (f32[2,1024,768]{2,1,0:T(8,128)}, f32[48,1152]{1,0:T(8,128)}, f32[48,384]{1,0:T(8,128)}, f32[2,144,128]{2,1,0:T(8,128)}, f32[8,128]{1,0:T(8,128)}, /*index=5*/f32[8,128]{1,0:T(8,128)}) custom-call(bf16[2048,768]{1,0:T(8,128)(2,1)} %tok_ref.3, bf16[2048,128]{1,0:T(8,128)(2,1)} %cond_ref.3, bf16[768,1024]{1,0:T(8,128)(2,1)} %get-tuple-element.81.h_in, ...), custom_call_target="tpu_custom_call" | custom-call | tf_op jit(solution)/shard_map/closing/pallas_call | solution.py:1584
  240.2 0.0 collective-permute-done.resb_ref
  240.2 0.0 copy-start
  240.2 1.1 copy-done
  241.4 10.9 %update_stage.1 = (f32[2048,768]{1,0:T(8,128)}, bf16[2048,768]{1,0:T(8,128)(2,1)}, f32[1,128]{1,0:T(1,128)}, f32[288,128]{1,0:T(8,128)}, f32[288,128]{1,0:T(8,12...) custom-call(s32[1]{0:T(128)} %bitcast.half, ...), custom_call_target="tpu_custom_call" | custom-call | tf_op jit(solution)/shard_map/update_stage/pallas_call | solution.py:1695
Async XLA Ops:
  125.5 114.7 %collective-permute-start = (bf16[1024,768]{1,0:T(8,128)(2,1)}, bf16[1024,768]{1,0:T(8,128)(2,1)S(1)}, u32[]{:S(2)}, u32[]{:S(2)}) collective-permute-start(bf16[1024,768]{1,0:T(8,128)(2,1)} %get-tuple-element.114.resa_ref), channel_id=1, source_target_pairs={{0,1},{1,0},{2,3},{3,2},{4,5},{5,4},{6,7},{7,6},{8,9},{9,8},{10,11... | collective-permute-start | bytes 4718600 | tf_op jit(solution)/shard_map/ppermute | solution.py:1725
  240.2 1.1 copy-start
